TPU v7x, 512 devices: a whole 4x8x8 slice. The times are simulated.
512 devices in a mesh: row: 16 (over z, y_lo), col: 4 (over x), seq: 8 (over y_hi, core).
Axes of the slice: x: 4, y: 8 (y_hi: 4, y_lo: 2; y = y_hi * 2 + y_lo), z: 8, core: 2. Of those that a mesh axis runs over, the one named last changes fastest.
Arguments:
- pair: bfloat16 [1024, 1024, 128], P(('row', 'seq'), 'col'), may hold values from -6 to 6
- alignment: bfloat16 [128, 1024, 256], P(('row', 'seq'), 'col'), may hold values from -6 to 6
- opm_left: bfloat16 [256, 32], replicated, may hold values from -0.375 to 0.375
- opm_right: bfloat16 [256, 32], replicated, may hold values from -0.375 to 0.375
- opm_out: bfloat16 [1024, 128], replicated, may hold values from -2 to 2
- tri_left: bfloat16 [128, 128], replicated, may hold values from -0.5 to 0.5
- tri_left_gate: bfloat16 [128, 128], replicated, may hold values from -0.5 to 0.5
- tri_right: bfloat16 [128, 128], replicated, may hold values from -0.5 to 0.5
- tri_right_gate: bfloat16 [128, 128], replicated, may hold values from -0.5 to 0.5
- tri_gate: bfloat16 [128, 128], replicated, may hold values from -0.5 to 0.5
- tri_out: bfloat16 [128, 128], replicated, may hold values from -0.5 to 0.5
Outputs:
- pair_out: bfloat16 [1024, 1024, 128], P(('row', 'seq'), 'col')
All inputs are finite; a program needn't handle non-finite values.
Results may differ from a plain program's by a relative error of at most 0.0075.
Values may be sent and summed in bfloat16 or wider, within the bound.
A program may use at most 64 MiB of HBM per device.

v0:
```python
import jax
import jax.numpy as jnp
from jax import lax
from jax.sharding import PartitionSpec as P

EPS = 1e-05


def spread_2(shard, axis, root):
    mine = lax.axis_index(axis) == root
    return lax.psum(jnp.where(mine, shard, jnp.zeros_like(shard)), axis)


def layer_norm(values, axis):
    values = values.astype(jnp.float32)
    center = values - jnp.mean(values, axis=axis, keepdims=True)
    spread = jnp.mean(center * center, axis=axis, keepdims=True)
    return center * lax.rsqrt(spread + EPS)


def contract(local_rows, piece):
    return jnp.einsum("cik,cjk->cij", local_rows, piece, preferred_element_type=jnp.float32)


def on_device(
    pair,
    alignment,
    opm_left,
    opm_right,
    opm_out,
    tri_left,
    tri_left_gate,
    tri_right,
    tri_right_gate,
    tri_gate,
    tri_out,
):
    rows_here, cols_here, pair_width = pair.shape
    seq_here = alignment.shape[0]
    model_width = alignment.shape[2]
    factor_width = opm_left.shape[1]
    hidden = tri_left.shape[1]
    n_row = lax.axis_size("row")
    n_col = lax.axis_size("col")
    n_seq = lax.axis_size("seq")
    seq_normed = (
        layer_norm(alignment, 2).astype(jnp.bfloat16).reshape(seq_here * cols_here, model_width)
    )
    left_proj = (
        jnp.dot(seq_normed, opm_left, preferred_element_type=jnp.float32)
        .astype(jnp.bfloat16)
        .reshape(seq_here, cols_here * factor_width)
    )
    right_proj = (
        jnp.dot(seq_normed, opm_right, preferred_element_type=jnp.float32)
        .astype(jnp.bfloat16)
        .reshape(seq_here, cols_here * factor_width)
    )
    per_col = n_row // n_col
    index_row = lax.axis_index("row")
    root_col = index_row // per_col
    left_all, right_all = (
        lax.all_gather(left_proj, ("row", "seq"), axis=0, tiled=True),
        lax.all_gather(right_proj, ("row", "seq"), axis=0, tiled=True),
    )
    index_seq = lax.axis_index("seq")
    offset = (index_row % per_col * n_seq + index_seq) * (rows_here * factor_width)
    row_slice = lax.dynamic_slice_in_dim(left_all, offset, rows_here * factor_width, 1)
    seqs_all = right_all.shape[0]
    row_factors = spread_2(row_slice, "col", root_col)
    right_wide = right_all.reshape(seqs_all, cols_here, factor_width)
    row_stack = jnp.swapaxes(row_factors.reshape(seqs_all, rows_here, factor_width), 0, 1)

    def outer_row(packed):
        row_vals, pair_row = packed
        outer_sum = jnp.einsum(
            "np,njq->jpq", row_vals, right_wide, preferred_element_type=jnp.float32
        )
        mean_outer = (
            (outer_sum * (1.0 / seqs_all))
            .astype(jnp.bfloat16)
            .reshape(cols_here, factor_width * factor_width)
        )
        return (
            pair_row.astype(jnp.float32)
            + jnp.dot(mean_outer, opm_out, preferred_element_type=jnp.float32)
        ).astype(jnp.bfloat16)

    pair_mid = lax.map(outer_row, (row_stack, pair))
    normed_pair = layer_norm(pair_mid, 2).astype(jnp.bfloat16)
    flat_pair = normed_pair.reshape(rows_here * cols_here, pair_width)

    def project(weight):
        return lax.dot_general(
            weight, flat_pair, (((0,), (1,)), ((), ())), preferred_element_type=jnp.float32
        )

    def gated(weight_gate, weight_value):
        gate_part = jax.nn.sigmoid(project(weight_gate))
        return (
            (gate_part * project(weight_value))
            .astype(jnp.bfloat16)
            .reshape(hidden, rows_here, cols_here)
        )

    left_first = gated(tri_left_gate, tri_left)
    right_first = gated(tri_right_gate, tri_right)
    left_local, right_local = (
        lax.all_to_all(
            lax.all_to_all(left_first, "col", split_axis=0, concat_axis=2, tiled=True),
            "seq",
            split_axis=0,
            concat_axis=1,
            tiled=True,
        ),
        lax.all_to_all(
            lax.all_to_all(right_first, "col", split_axis=0, concat_axis=2, tiled=True),
            "seq",
            split_axis=0,
            concat_axis=1,
            tiled=True,
        ),
    )
    product = contract(left_local, lax.all_gather(right_local, "row", axis=1, tiled=True))
    product = product.astype(jnp.bfloat16)
    returned = lax.all_to_all(
        lax.all_to_all(product, "col", split_axis=2, concat_axis=0, tiled=True),
        "seq",
        split_axis=1,
        concat_axis=0,
        tiled=True,
    )
    per_group = hidden // (n_col * n_seq)
    weights_order = (
        tri_out.reshape(n_col, n_seq, per_group, pair_width)
        .transpose(1, 0, 2, 3)
        .reshape(hidden, pair_width)
    )
    normed_product = layer_norm(returned, 0).astype(jnp.bfloat16)
    update = jnp.einsum(
        "cij,cd->ijd", normed_product, weights_order, preferred_element_type=jnp.float32
    )
    gate_part = jax.nn.sigmoid(
        jnp.dot(flat_pair, tri_gate, preferred_element_type=jnp.float32)
    ).reshape(rows_here, cols_here, pair_width)
    return (pair_mid.astype(jnp.float32) + gate_part * update).astype(jnp.bfloat16)


def solution(mesh):
    return jax.shard_map(
        on_device,
        mesh=mesh,
        in_specs=(
            P(("row", "seq"), "col", None),
            P(("row", "seq"), "col", None),
            P(),
            P(),
            P(),
            P(),
            P(),
            P(),
            P(),
            P(),
            P(),
        ),
        out_specs=P(("row", "seq"), "col", None),
        check_vma=False,
    )
```

profile of v0, /device:TPU:1, one launch (start us, length us, event | category | flops | bytes accessed | tf_op | source)
XLA Modules:
  0.0 816.8 jit_solution(16406924209503788000)
XLA Ops:
  6.5 1.0 convert_reduce_fusion.1
  7.6 1.1 fusion.35
  8.7 1.2 convolution_convert_fusion.2
  10.0 0.7 reshape.100
  10.8 1.2 convolution_convert_fusion.1
  12.1 0.7 reshape.102
  12.9 222.8 %all-gather.8.cloned.1.call-done = bf16[128,1,8192]{2,1,0:T(2,128)(2,1)} async-done(((bf16[1,1,8192]{2,1,0:T(2,128)(2,1)}), bf16[128,1,8192]{2,1,0:T(2,128)(2,1)}) %all-gather.8.cloned.1.call-update) | async-done | bytes 2097168 | tf_op jit(solution)/shard_map/all_gather | solution.py:63
  235.7 1.0 constant_dynamic-slice_fusion
  236.8 0.6 broadcast_select_fusion
  237.6 218.4 %all-gather.10.cloned.1.call-done = bf16[128,1,8192]{2,1,0:T(2,128)(2,1)} async-done(((bf16[1,1,8192]{2,1,0:T(2,128)(2,1)}), bf16[128,1,8192]{2,1,0:T(2,128)(2,1)}) %all-gather.10.cloned.1.call-update) | async-done | bytes 2097168 | tf_op jit(solution)/shard_map/all_gather | solution.py:64
  456.0 9.1 %copy.67 = bf16[128,1,8192]{0,2,1:T(8,128)(2,1)} copy(bf16[128,1,8192]{2,1,0:T(2,128)(2,1)} %all-gather.10.cloned.1.call-done) | data formatting | bytes 4194304 | tf_op jit(solution)/shard_map/all_gather | solution.py:64
  465.1 3.0 copy.68
  468.1 38.8 %all-reduce.2.cloned.1.call-done = bf16[8,128,32]{1,2,0:T(8,128)(2,1)} async-done(((bf16[8,128,32]{1,2,0:T(8,128)(2,1)}), bf16[8,128,32]{1,2,0:T(8,128)(2,1)}) %all-reduce.2.cloned.1.call-update) | async-done | bytes 65552 | tf_op jit(solution)/shard_map/psum | solution.py:11
  506.9 21.1 %while.10 = (s32[]{:T(128)}, bf16[8,256,128]{2,1,0:T(8,128)(2,1)S(1)}, bf16[8,256,128]{2,1,0:T(8,128)(2,1)}, bf16[8,128,32]{1,2,0:T(8,128)(2,1)}, bf16[128,256,3...) while((s32[]{:T(128)}, bf16[8,256,128]{2,1,0:T(8,128)(2,1)S(1)}, ...), condition=%wide.region_4.5_spmd, body=%wide.region_3.4_spmd.sunk | while | flops 134840320 | bytes 4596305 | solution.py:89
  506.9 1.1 fusion.67
  508.0 0.3 copy.100
  508.3 1.2 fusion.68
  509.6 1.1 fusion.67
  510.7 0.3 copy.100
  511.0 1.2 fusion.68
  512.2 1.1 fusion.67
  513.3 0.3 copy.100
  513.6 1.2 fusion.68
  514.9 1.1 fusion.67
  516.0 0.3 copy.100
  516.3 1.2 fusion.68
  517.5 1.1 fusion.67
  518.6 0.3 copy.100
  518.9 1.2 fusion.68
  520.2 1.1 fusion.67
  521.3 0.3 copy.100
  521.6 1.2 fusion.68
  522.8 1.1 fusion.67
  523.9 0.3 copy.100
  524.2 1.2 fusion.68
  525.4 1.1 fusion.67
  526.6 0.3 copy.100
  526.9 1.2 fusion.68
  528.3 0.6 fusion.22
  529.0 0.6 fusion.23
  529.6 0.4 fusion.10
  530.0 0.3 fusion.18
  530.3 0.4 copy.72
  530.7 10.1 %all_to_all.99 = bf16[128,8,256]{2,1,0:T(8,128)(2,1)S(1)} all-to-all(bf16[128,8,256]{2,1,0:T(8,128)(2,1)S(1)} %copy.72), channel_id=1, replica_groups=mesh['row'=16,'col'=4,'seq'=8] {'col'}, dimensions={0} | all-to-all | bytes 1048576 | tf_op jit(solution)/shard_map/all_to_all | solution.py:117
  540.9 26.4 %all_to_all.100 = bf16[32,8,1024]{2,1,0:T(8,128)(2,1)S(1)} all-to-all(bf16[32,8,1024]{2,1,0:T(8,128)(2,1)S(1)} %bitcast.131), channel_id=1, replica_groups=mesh['row'=16,'col'=4,'seq'=8] {'seq'}, dimensions={0} | all-to-all | bytes 1048576 | tf_op jit(solution)/shard_map/all_to_all | solution.py:116
  567.4 0.8 copy.98
  568.2 0.4 fusion.13
  568.7 0.3 fusion.17
  568.9 0.4 copy.69
  569.3 10.3 %all_to_all.101 = bf16[128,8,256]{2,1,0:T(8,128)(2,1)S(1)} all-to-all(bf16[128,8,256]{2,1,0:T(8,128)(2,1)S(1)} %copy.69), channel_id=1, replica_groups=mesh['row'=16,'col'=4,'seq'=8] {'col'}, dimensions={0} | all-to-all | bytes 1048576 | tf_op jit(solution)/shard_map/all_to_all | solution.py:110
  579.7 27.8 %all_to_all.102 = bf16[32,8,1024]{2,1,0:T(8,128)(2,1)S(1)} all-to-all(bf16[32,8,1024]{2,1,0:T(8,128)(2,1)S(1)} %bitcast.134), channel_id=1, replica_groups=mesh['row'=16,'col'=4,'seq'=8] {'seq'}, dimensions={0} | all-to-all | bytes 1048576 | tf_op jit(solution)/shard_map/all_to_all | solution.py:109
  607.5 155.4 %all-gather.6.cloned.1.call-done = bf16[4,1024,1024]{2,1,0:T(8,128)(2,1)} async-done(((bf16[4,64,1024]{2,1,0:T(8,128)(2,1)}), bf16[4,1024,1024]{2,1,0:T(8,128)(2,1)}) %all-gather.6.cloned.1.call-update) | async-done | bytes 8388624 | tf_op jit(solution)/shard_map/all_gather | solution.py:124
  762.9 6.0 convolution_convert_fusion
  768.9 0.7 copy.75
  769.7 0.9 reshape.114
  770.6 11.6 %all_to_all.103 = bf16[4,2,32768]{2,1,0:T(2,128)(2,1)S(1)} all-to-all(bf16[4,2,32768]{2,1,0:T(2,128)(2,1)S(1)} %reshape.114), channel_id=1, replica_groups=mesh['row'=16,'col'=4,'seq'=8] {'col'}, dimensions={0} | all-to-all | bytes 1048576 | tf_op jit(solution)/shard_map/all_to_all | solution.py:127
  782.1 0.7 reshape.115
  782.9 0.5 copy.77
  783.4 1.1 copy.78
  784.5 8.4 %all-to-all-start.5 = ((bf16[16,64,256]{2,0,1:T(8,128)(2,1)}), bf16[16,64,256]{2,0,1:T(8,128)(2,1)S(1)}, u32[]{:S(2)}, u32[]{:S(2)}) async-start(bf16[16,64,256]{2,0,1:T(8,128)(2,1)} %copy.78), calls=%async_computation.5 | async-start | bytes 1048576 | tf_op jit(solution)/shard_map/all_to_all | solution.py:126
  793.0 0.4 fusion.16
  793.4 15.1 %all-to-all-done.5 = bf16[16,64,256]{2,0,1:T(8,128)(2,1)S(1)} async-done(((bf16[16,64,256]{2,0,1:T(8,128)(2,1)}), bf16[16,64,256]{2,0,1:T(8,128)(2,1)S(1)}, u32[]{:S(2)}, u32[]{:S(2)}) %all-to-all-start.5) | async-done | bytes 524320 | tf_op jit(solution)/shard_map/all_to_all | solution.py:126
  808.7 0.2 fusion.28
  809.2 1.1 fusion.19
  (39 shorter events, 1.4 us)
Async XLA Ops:
  6.5 523.0 %copy-start = (bf16[128,128]{1,0:T(8,128)(2,1)S(1)}, bf16[128,128]{1,0:T(8,128)(2,1)}, u32[]{:S(2)}) copy-start(bf16[128,128]{1,0:T(8,128)(2,1)} %param.21) | copy-start | bytes 98308
  6.5 229.1 %all-gather.8.cloned.1.call-start = ((), (), s32[]{:S(2)}) async-start(), calls=%async_computation.8 | async-start | bytes 4227072 | tf_op jit(solution)/shard_map/all_gather | solution.py:63
  10.7 445.3 %all-gather.10.cloned.1.call-start = ((), (), s32[]{:S(2)}) async-start(), calls=%async_computation.9 | async-start | bytes 4227072 | tf_op jit(solution)/shard_map/all_gather | solution.py:64
  12.8 494.1 %all-reduce.2.cloned.1.call-start = ((), (), s32[]{:S(2)}) async-start(), calls=%async_computation.6 | async-start | bytes 131072 | tf_op jit(solution)/shard_map/psum | solution.py:11
  237.5 525.4 %all-gather.6.cloned.1.call-start = ((), (), s32[]{:S(2)}) async-start(), calls=%async_computation.7 | async-start | bytes 8912896 | tf_op jit(solution)/shard_map/all_gather | solution.py:124
  237.6 269.4 %copy-start.1 = (bf16[1024,128]{1,0:T(8,128)(2,1)S(1)}, bf16[1024,128]{1,0:T(8,128)(2,1)}, u32[]{:S(2)}) copy-start(bf16[1024,128]{1,0:T(8,128)(2,1)} %param.17) | copy-start | bytes 786436
  528.1 1.9 copy-start.2
  530.0 38.2 %copy-start.5 = (bf16[128,128]{1,0:T(8,128)(2,1)S(1)}, bf16[128,128]{1,0:T(8,128)(2,1)}, u32[]{:S(2)}) copy-start(bf16[128,128]{1,0:T(8,128)(2,1)} %param.19) | copy-start | bytes 98308
  540.8 27.8 %copy-start.3 = (bf16[128,128]{1,0:T(8,128)(2,1)S(1)}, bf16[128,128]{1,0:T(8,128)(2,1)}, u32[]{:S(2)}) copy-start(bf16[128,128]{1,0:T(8,128)(2,1)} %param.18) | copy-start | bytes 98308
  769.7 23.3 %copy-start.4 = (bf16[128,128]{1,0:T(8,128)(2,1)S(1)}, bf16[128,128]{1,0:T(8,128)(2,1)}, u32[]{:S(2)}) copy-start(bf16[128,128]{1,0:T(8,128)(2,1)} %param.23) | copy-start | bytes 98308
  769.7 23.3 %copy-start.6 = (bf16[128,128]{1,0:T(8,128)(2,1)S(1)}, bf16[128,128]{1,0:T(8,128)(2,1)}, u32[]{:S(2)}) copy-start(bf16[128,128]{1,0:T(8,128)(2,1)} %param.22) | copy-start | bytes 98308
  784.5 24.0 %all-to-all-start.5 = ((bf16[16,64,256]{2,0,1:T(8,128)(2,1)}), bf16[16,64,256]{2,0,1:T(8,128)(2,1)S(1)}, u32[]{:S(2)}, u32[]{:S(2)}) async-start(bf16[16,64,256]{2,0,1:T(8,128)(2,1)} %copy.78), calls=%async_computation.5 | async-start | bytes 1048576 | tf_op jit(solution)/shard_map/all_to_all | solution.py:126
Sparse Core Ops, SparseCore 0:
  10.8 224.7 all-gather.7
  237.8 218.1 all-gather.9
  458.3 48.5 all-reduce.1
  568.3 194.5 all-gather.5
where the time goes:
time: 819 us; the launch traced here: 817 us
  waiting for transfers between devices  651 us (79%)
  blocking collectives  86.2 us (11%)
  matrix products  29.9 us (4%)
  local copies, waits for them, and re-layouts  23.1 us (3%)
  between operations  13.5 us (2%)
  starting transfers between devices  8.57 us (1%)
    all_gather x1, waiting for transfers between devices, on_device(): lax.all_gather(left_proj, ('row', 'seq'), axis=0, tiled=True)  223 us
    all_gather x1, waiting for transfers between devices, on_device(): lax.all_gather(right_proj, ('row', 'seq'), axis=0, tiled=True)  218 us
    all_gather x1, waiting for transfers between devices, on_device(): lax.all_gather(right_local, 'row', axis=1, tiled=True)  155 us
    psum x1, waiting for transfers between devices, spread_2(): return lax.psum(jnp.where(mine, shard, jnp.zeros_like(shard)), axis)  38.8 us
    all_to_all x1, blocking collectives, on_device(): lax.all_to_all(lax.all_to_all(left_first, 'col', split_axis=0, concat_axi...  27.8 us
    all_to_all x1, blocking collectives, on_device(): lax.all_to_all(lax.all_to_all(right_first, 'col', split_axis=0, concat_ax...  26.4 us
  transfers between devices with their start and end apart: 5, of which 5 were waited for; matrix products, arithmetic and copies ran while one was open for 2% of the time, Pallas kernels for 0%

commit v1 on v0

v1 whole, which is shorter than its diff:
```python
import functools

import jax
import jax.numpy as jnp
from jax import lax
from jax.experimental import pallas as pl
from jax.experimental.pallas import tpu as pltpu
from jax.sharding import PartitionSpec as P

EPS = 1e-05
MESH = pl.DeviceIdType.MESH
F32 = jnp.float32
BF16 = jnp.bfloat16
VMEM = pl.BlockSpec(memory_space=pltpu.VMEM)
ANY = pl.BlockSpec(memory_space=pl.ANY)
DMA = pltpu.SemaphoreType.DMA

NX = 4
NZ = 8
NQ = 8
NS = 2 * NQ
NY = NS // 2
HOPS = (1, 7, 2, 6, 3, 5, 4)


class Place:
    def __init__(self):
        row = lax.axis_index("row")
        self.x = lax.axis_index("col")
        seq = lax.axis_index("seq")
        self.z = row // 2
        self.s = (row % 2) * NQ + seq
        self.yy = self.s // 2
        self.core = self.s % 2

    def at(self, z=None, s=None, x=None):
        z = self.z if z is None else z
        s = self.s if s is None else s
        x = self.x if x is None else x
        return (z * 2 + s // NQ, x, s % NQ)


def send(src, dst, send_sem, recv_sem, device):
    pltpu.make_async_remote_copy(
        src_ref=src,
        dst_ref=dst,
        send_sem=send_sem,
        recv_sem=recv_sem,
        device_id=device,
        device_id_type=MESH,
    ).start()


def keep(src, dst, sem):
    pltpu.make_async_copy(src, dst, sem).start()


def await_bytes(ref, sem):
    pltpu.make_async_copy(ref, ref, sem).wait()


def greet(device):
    pl.semaphore_signal(
        pltpu.get_barrier_semaphore(), inc=1, device_id=device, device_id_type=MESH
    )


def greet_plane(me):
    for t in range(1, NS):
        greet(me.at(s=(me.s + t) % NS))
    for t in range(1, NZ):
        greet(me.at(z=(me.z + t) % NZ))
    return NS - 1 + NZ - 1


def layer_norm(values, axis):
    values = values.astype(F32)
    center = values - jnp.mean(values, axis=axis, keepdims=True)
    spread = jnp.mean(center * center, axis=axis, keepdims=True)
    return center * lax.rsqrt(spread + EPS)


def gather_kernel(
    right_ref, left_ref, all_ref, mine_ref, half_ref, send_sem, first_sem, next_sem, twin_sem, left_sem
):
    me = Place()
    z, s, x, yy, core = me.z, me.s, me.x, me.yy, me.core
    owner = z // 2

    count = greet_plane(me)
    for t in range(NZ):

        @pl.when(jnp.logical_not(jnp.logical_and(owner == x, z == t)))
        def _():
            greet(me.at(z=t, x=owner))

    here = jnp.where(owner == x, 1, 0)
    pl.semaphore_wait(pltpu.get_barrier_semaphore(), count + 8 - here)

    for h in range(2):
        for xt in range(NX):
            zt = 2 * x + h
            same = jnp.logical_and(x == xt, z == zt)

            @pl.when(same)
            def _():
                keep(left_ref.at[h], half_ref.at[z], left_sem.at[0])

            @pl.when(jnp.logical_not(same))
            def _():
                send(
                    left_ref.at[h], half_ref.at[z], send_sem.at[0], left_sem.at[0], me.at(z=zt, x=xt)
                )

    own = all_ref.at[z, yy, core]
    keep(right_ref, own, first_sem)

    @pl.when(core == 0)
    def _():
        for t in HOPS:
            send(right_ref, own, send_sem.at[1], first_sem, me.at(z=(z + t) % NZ))

    @pl.when(core == 1)
    def _():
        for t in HOPS:
            send(right_ref, own, send_sem.at[1], first_sem, me.at(s=(s + 2 * t) % NS))

    await_bytes(half_ref, left_sem.at[0])
    keep(half_ref.at[:, s], mine_ref.at[:, s], left_sem.at[1])
    for t in range(1, NS):
        st = (s + t) % NS
        send(half_ref.at[:, st], mine_ref.at[:, s], send_sem.at[2], left_sem.at[1], me.at(s=st))

    await_bytes(all_ref.at[:, 0, 0], first_sem)
    twin = me.at(s=s + 1 - 2 * core)

    @pl.when(core == 0)
    def _():
        line = all_ref.at[:, yy, 0]
        for t in HOPS:
            send(line, line, send_sem.at[3], next_sem.at[yy], me.at(s=(s + 2 * t) % NS))
        send(line, line, send_sem.at[4], twin_sem.at[yy], twin)
        for t in HOPS:
            yt = (yy + t) % NY
            part = all_ref.at[:, yt, 0]
            await_bytes(part, next_sem.at[yt])
            send(part, part, send_sem.at[4], twin_sem.at[yt], twin)

    @pl.when(core == 1)
    def _():
        line = all_ref.at[z, :, 1]
        for t in HOPS:
            send(line, line, send_sem.at[3], next_sem.at[z], me.at(z=(z + t) % NZ))
        send(line, line, send_sem.at[4], twin_sem.at[z], twin)
        for t in HOPS:
            zt = (z + t) % NZ
            part = all_ref.at[zt, :, 1]
            await_bytes(part, next_sem.at[zt])
            send(part, part, send_sem.at[4], twin_sem.at[zt], twin)

    for t in range(8):
        await_bytes(all_ref.at[:, 0, 0], twin_sem.at[t])
    await_bytes(mine_ref, left_sem.at[1])

    @pl.when(here == 1)
    def _():
        await_bytes(half_ref.at[pl.ds(0, 7)], send_sem.at[0])

    @pl.when(here == 0)
    def _():
        await_bytes(half_ref, send_sem.at[0])

    await_bytes(all_ref.at[pl.ds(0, 7), 0, 0], send_sem.at[1])
    await_bytes(mine_ref.at[:, pl.ds(0, NS - 1)], send_sem.at[2])
    await_bytes(all_ref.at[pl.ds(0, 7), :, 0], send_sem.at[3])
    await_bytes(all_ref.at[:, :, 0], send_sem.at[4])


def gather_factors(right, left):
    q, cols = right.shape
    pair = left.shape[2:]
    return pl.pallas_call(
        gather_kernel,
        out_shape=(
            jax.ShapeDtypeStruct((NZ, NY, 2, q, cols), BF16),
            jax.ShapeDtypeStruct((NZ, NS) + pair, BF16),
        ),
        in_specs=[VMEM, VMEM],
        out_specs=(ANY, ANY),
        scratch_shapes=[
            pltpu.VMEM((NZ, NS) + pair, BF16),
            DMA((5,)),
            DMA,
            DMA((8,)),
            DMA((8,)),
            DMA((2,)),
        ],
        compiler_params=pltpu.CompilerParams(collective_id=0, has_side_effects=True),
        name="gather_factors",
    )(right, left)


def first_legs(me, a_in, b_in, a_mid, b_mid, send_sem, a_sem, b_sem):
    z, s = me.z, me.s
    keep(a_in.at[:, s], a_mid.at[s], a_sem)
    keep(b_in.at[z], b_mid.at[z], b_sem)
    for t in range(1, NS):
        st = (s + t) % NS
        send(a_in.at[:, st], a_mid.at[s], send_sem.at[0], a_sem, me.at(s=st))
        if t <= len(HOPS):
            zt = (z + HOPS[t - 1]) % NZ
            send(b_in.at[zt], b_mid.at[z], send_sem.at[1], b_sem, me.at(z=zt))


def sent_legs(a_mid, b_mid, send_sem):
    await_bytes(a_mid.at[pl.ds(0, NS - 1)], send_sem.at[0])
    await_bytes(b_mid.at[pl.ds(0, NZ - 1)], send_sem.at[1])
    await_bytes(a_mid.at[:, pl.ds(0, NZ - 1)], send_sem.at[2])
    await_bytes(b_mid.at[:, pl.ds(0, NS - 1)], send_sem.at[3])


def spread_kernel(
    a_in,
    b_in,
    a_out,
    b_out,
    a_mid,
    b_mid,
    b_all,
    send_sem,
    first_sem,
    a_sem,
    b_sem,
    right_sem,
    left_sem,
    far_sem,
    side_sem,
):
    me = Place()
    z, s, x = me.z, me.s, me.x
    count = greet_plane(me)
    for t in range(1, NX):
        greet(me.at(x=(x + t) % NX))
    pl.semaphore_wait(pltpu.get_barrier_semaphore(), count + NX - 1)

    first_legs(me, a_in, b_in, a_mid, b_mid, send_sem, first_sem.at[0], first_sem.at[1])
    await_bytes(a_mid, first_sem.at[0])
    keep(a_mid.at[:, z], a_out.at[x, z], a_sem.at[z])
    for t in HOPS:
        zt = (z + t) % NZ
        send(a_mid.at[:, zt], a_out.at[x, z], send_sem.at[2], a_sem.at[z], me.at(z=zt))
    await_bytes(b_mid, first_sem.at[1])
    keep(b_mid.at[:, s], b_all.at[:, s], b_sem)
    for t in range(1, NS):
        st = (s + t) % NS
        send(b_mid.at[:, st], b_all.at[:, s], send_sem.at[3], b_sem, me.at(s=st))

    after, before = (x + 1) % NX, (x + 3) % NX

    def pass_on(t):
        zt = (z + t) % NZ
        if t in (0, 5, 6, 7):
            part = a_out.at[before, zt]
            await_bytes(part, left_sem.at[zt])
            send(part, part, send_sem.at[5], far_sem.at[zt], me.at(x=after))
        else:
            part = a_out.at[after, zt]
            await_bytes(part, right_sem.at[zt])
            send(part, part, send_sem.at[5], far_sem.at[zt], me.at(x=before))

    order = (0,) + HOPS
    for k, t in enumerate(order):
        zt = (z + t) % NZ
        part = a_out.at[x, zt]
        await_bytes(part, a_sem.at[zt])
        send(part, part, send_sem.at[4], left_sem.at[zt], me.at(x=after))
        send(part, part, send_sem.at[4], right_sem.at[zt], me.at(x=before))
        if k >= 2:
            pass_on(order[k - 2])
    await_bytes(b_all, b_sem)
    keep(b_all.at[pl.ds(2 * x, 2)], b_out.at[x], side_sem)
    for t in range(1, NX):
        xt = (x + t) % NX
        send(b_all.at[pl.ds(2 * xt, 2)], b_out.at[x], send_sem.at[6], side_sem, me.at(x=xt))
    for t in order[-2:]:
        pass_on(t)
    for t in order:
        zt = (z + t) % NZ
        await_bytes(a_out.at[x, zt], far_sem.at[zt])
        await_bytes(a_out.at[x, zt], (right_sem if t in (0, 5, 6, 7) else left_sem).at[zt])
    await_bytes(b_out, side_sem)

    sent_legs(a_mid, b_mid, send_sem)
    await_bytes(a_out.at[pl.ds(0, 2)], send_sem.at[4])
    await_bytes(a_out.at[0], send_sem.at[5])
    await_bytes(b_out.at[pl.ds(0, NX - 1)], send_sem.at[6])


def spread_triangle(left, right):
    rows, cols = left.shape[2:]
    return pl.pallas_call(
        spread_kernel,
        out_shape=(
            jax.ShapeDtypeStruct((NX, NZ, NS, rows, cols), BF16),
            jax.ShapeDtypeStruct((NX, NZ // NX, NS, rows, cols), BF16),
        ),
        in_specs=[VMEM, VMEM],
        out_specs=(ANY, ANY),
        scratch_shapes=[
            pltpu.VMEM((NS, NZ, rows, cols), BF16),
            pltpu.VMEM((NZ, NS, rows, cols), BF16),
            pltpu.VMEM((NZ, NS, rows, cols), BF16),
            DMA((7,)),
            DMA((2,)),
            DMA((NZ,)),
            DMA,
            DMA((NZ,)),
            DMA((NZ,)),
            DMA((NZ,)),
            DMA,
        ],
        compiler_params=pltpu.CompilerParams(collective_id=1, has_side_effects=True),
        name="spread_triangle",
    )(left, right)


def return_kernel(a_in, b_in, a_out, b_out, a_mid, b_mid, send_sem, first_sem, last_sem):
    me = Place()
    z, s = me.z, me.s
    pl.semaphore_wait(pltpu.get_barrier_semaphore(), greet_plane(me))

    first_legs(me, a_in, b_in, a_mid, b_mid, send_sem, first_sem.at[0], first_sem.at[1])
    await_bytes(a_mid, first_sem.at[0])
    keep(a_mid.at[:, z], a_out.at[z], last_sem.at[0])
    for t in HOPS:
        zt = (z + t) % NZ
        send(a_mid.at[:, zt], a_out.at[z], send_sem.at[2], last_sem.at[0], me.at(z=zt))
    await_bytes(b_mid, first_sem.at[1])
    keep(b_mid.at[:, s], b_out.at[:, s], last_sem.at[1])
    for t in range(1, NS):
        st = (s + t) % NS
        send(b_mid.at[:, st], b_out.at[:, s], send_sem.at[3], last_sem.at[1], me.at(s=st))
    await_bytes(a_out, last_sem.at[0])
    await_bytes(b_out, last_sem.at[1])
    sent_legs(a_mid, b_mid, send_sem)


def return_product(a, b):
    rows, cols = a.shape[2:]
    out = jax.ShapeDtypeStruct((NZ, NS, rows, cols), BF16)
    return pl.pallas_call(
        return_kernel,
        out_shape=(out, out),
        in_specs=[VMEM, VMEM],
        out_specs=(ANY, ANY),
        scratch_shapes=[
            pltpu.VMEM((NS, NZ, rows, cols), BF16),
            pltpu.VMEM((NZ, NS, rows, cols), BF16),
            DMA((4,)),
            DMA((2,)),
            DMA((2,)),
        ],
        compiler_params=pltpu.CompilerParams(collective_id=2, has_side_effects=True),
        name="return_product",
    )(a, b)


def turned(ref):
    return ref[...].astype(F32).T.astype(BF16)


def sigmoid(x):
    return jax.nn.sigmoid(x)


def outer_kernel(
    seqs,
    left_ref,
    right_ref,
    out_ref,
    pair_ref,
    wl_ref,
    wlg_ref,
    wr_ref,
    wrg_ref,
    left_out,
    right_out,
    mid_out,
    normed_out,
    wide,
    stack,
    left_acc,
    right_acc,
):
    rows, cols, width = pair_ref.shape
    factor = left_ref.shape[0] // rows
    halves = cols // 128

    @pl.loop(0, seqs // 8)
    def _(k):
        at = pl.ds(pl.multiple_of(k * 8 * factor, 8 * factor), 8 * factor)
        for h in range(halves):
            wide[h, at, :] = right_ref[at, h * 128 : (h + 1) * 128].astype(F32)

    @pl.loop(0, factor)
    def _(q):
        part = jnp.concatenate(
            [wide[h, pl.ds(q, seqs, stride=factor), :] for h in range(halves)], axis=1
        ).astype(BF16)
        outer = jnp.dot(left_ref[...], part, preferred_element_type=F32) * (1.0 / seqs)
        at = pl.ds(pl.multiple_of(q * factor, factor), factor)
        stack[:, at, :] = outer.astype(BF16).reshape(rows, factor, cols)

    wl, wlg, wr, wrg = turned(wl_ref), turned(wlg_ref), turned(wr_ref), turned(wrg_ref)
    hidden = wl.shape[0]

    @pl.loop(0, rows)
    def _(i):
        mid = (
            jnp.dot(out_ref[...], stack[i], preferred_element_type=F32)
            + pair_ref[i].astype(F32).T
        ).astype(BF16)
        mid_out[i] = mid
        normed = layer_norm(mid, 0).astype(BF16)
        normed_out[i] = normed

        def project(weight):
            return jnp.dot(weight, normed, preferred_element_type=F32)

        left = sigmoid(project(wlg)) * project(wl)
        right = sigmoid(project(wrg)) * project(wr)
        for h in range(halves):
            lanes = slice(h * 128, (h + 1) * 128)
            left_acc[h, pl.ds(i, hidden, stride=rows), :] = left[:, lanes]
            right_acc[h, pl.ds(i, hidden, stride=rows), :] = right[:, lanes]

    for h in range(halves):
        lanes = slice(h * 128, (h + 1) * 128)
        left_out[:, :, lanes] = left_acc[h].reshape(hidden, rows, 128).astype(BF16)
        right_out[:, :, lanes] = right_acc[h].reshape(hidden, rows, 128).astype(BF16)


def outer_and_gates(left, right, out, pair, wl, wlg, wr, wrg):
    rows, cols, width = pair.shape
    hidden = wl.shape[1]
    depth = right.shape[0]
    factor = left.shape[0] // rows
    chan = jax.ShapeDtypeStruct((hidden, rows, cols), BF16)
    flat = jax.ShapeDtypeStruct((rows, width, cols), BF16)
    return pl.pallas_call(
        functools.partial(outer_kernel, depth // factor),
        out_shape=(chan, chan, flat, flat),
        in_specs=[VMEM] * 8,
        out_specs=(VMEM,) * 4,
        scratch_shapes=[
            pltpu.VMEM((cols // 128, depth, 128), F32),
            pltpu.VMEM((rows, factor * factor, cols), BF16),
            pltpu.VMEM((cols // 128, hidden * rows, 128), F32),
            pltpu.VMEM((cols // 128, hidden * rows, 128), F32),
        ],
        compiler_params=pltpu.CompilerParams(vmem_limit_bytes=48 << 20),
        name="outer_and_gates",
    )(left, right, out, pair, wl, wlg, wr, wrg)


def final_kernel(a_ref, b_ref, mid_ref, normed_ref, gate_ref, out_w_ref, out_ref, wide):
    rows, width, cols = mid_ref.shape
    hidden = a_ref.shape[0]
    for h, ref in enumerate((a_ref, b_ref)):
        wide[h] = ref[...].astype(F32).reshape(hidden * rows, 128)
    gate_w, out_w = turned(gate_ref), turned(out_w_ref)

    @pl.loop(0, rows)
    def _(i):
        product = jnp.concatenate(
            [wide[h, pl.ds(i, hidden, stride=rows), :] for h in range(2)], axis=1
        )
        normed = layer_norm(product, 0).astype(BF16)
        update = jnp.dot(out_w, normed, preferred_element_type=F32)
        gate = sigmoid(jnp.dot(gate_w, normed_ref[i], preferred_element_type=F32))
        out_ref[i] = (mid_ref[i].astype(F32) + gate * update).T.astype(BF16)


def final_update(a, b, mid, normed, gate, out_w):
    rows, width, cols = mid.shape
    hidden = a.shape[0]
    return pl.pallas_call(
        final_kernel,
        out_shape=jax.ShapeDtypeStruct((rows, cols, width), BF16),
        in_specs=[VMEM] * 6,
        out_specs=VMEM,
        scratch_shapes=[pltpu.VMEM((2, hidden * rows, 128), F32)],
        compiler_params=pltpu.CompilerParams(vmem_limit_bytes=32 << 20),
        name="final_update",
    )(a, b, mid, normed, gate, out_w)


def on_device(
    pair,
    alignment,
    opm_left,
    opm_right,
    opm_out,
    tri_left,
    tri_left_gate,
    tri_right,
    tri_right_gate,
    tri_gate,
    tri_out,
):
    rows, cols, width = pair.shape
    factor = opm_left.shape[1]
    hidden = tri_left.shape[1]
    seqs = NZ * NS

    seq_normed = layer_norm(alignment[0], 1).astype(BF16)
    left = jnp.dot(seq_normed, opm_left, preferred_element_type=F32).astype(BF16)
    right = lax.dot_general(
        opm_right, seq_normed, (((0,), (1,)), ((), ())), preferred_element_type=F32
    ).astype(BF16)
    right_all, left_mine = gather_factors(right, left.reshape(2, NS, 2, rows * factor // 2))
    left_rows = left_mine.reshape(seqs, rows * factor).T
    out_w = opm_out.reshape(factor, factor, width).transpose(2, 1, 0).reshape(width, -1)
    left_tri, right_tri, mid, normed = outer_and_gates(
        left_rows,
        right_all.reshape(seqs * factor, cols),
        out_w,
        pair,
        tri_left,
        tri_left_gate,
        tri_right,
        tri_right_gate,
    )
    blocks = (NZ, NS, rows, cols)
    left_all, right_here = spread_triangle(left_tri.reshape(blocks), right_tri.reshape(blocks))
    residues = NZ * NS * rows
    product = jnp.einsum(
        "xik,xjk->ij",
        left_all.reshape(NX, residues, cols),
        right_here.reshape(NX, cols, cols),
        preferred_element_type=F32,
    ).astype(BF16)
    half = (NZ, NS, rows, cols // 2)
    a, b = return_product(
        product[:, : cols // 2].reshape(half), product[:, cols // 2 :].reshape(half)
    )
    chan = (hidden, rows, cols // 2)
    return final_update(a.reshape(chan), b.reshape(chan), mid, normed, tri_gate, tri_out)


def solution(mesh):
    split = P(("row", "seq"), "col", None)
    return jax.shard_map(
        on_device,
        mesh=mesh,
        in_specs=(split, split) + (P(),) * 9,
        out_specs=split,
        check_vma=False,
    )
```

time: 819 us -> 150 us (0.18)
  waiting for transfers between devices: 651 us -> 0 us
  Pallas kernels: 0 us -> 133 us
  blocking collectives: 86.2 us -> 0 us
  matrix products: 29.9 us -> 5.35 us
  local copies, waits for them, and re-layouts: 23.1 us -> 8.93 us
  between operations: 13.5 us -> 0.21 us
  starting transfers between devices: 8.57 us -> 0 us
    all_gather x3 -> x0, waiting for transfers between devices: 597 us -> none  [the longest x1 223 us: on_device(): lax.all_gather(left_proj, ('row', 'seq'), axis=0, tiled=True)]
    pallas_call x0 -> x5, Pallas kernels: none -> 133 us  [the longest x1 50.1 us: spread_triangle(): pl.pallas_call(spread_kernel, out_shape=(jax.ShapeDtypeStruct((NX, NZ, NS...]
    all_to_all x5 -> x0, blocking collectives: 86.2 us -> none  [the longest x1 27.8 us: on_device(): lax.all_to_all(lax.all_to_all(left_first, 'col', split_axis=0, concat_axi...]
    psum x1 -> x0, waiting for transfers between devices: 38.8 us -> none  [spread_2(): return lax.psum(jnp.where(mine, shard, jnp.zeros_like(shard)), axis)]
    dot_general x25 -> x3, matrix products: 29.9 us -> 5.35 us  [the longest x1 2.42 us: on_device(): jnp.einsum('xik,xjk->ij', left_all.reshape(NX, residues, cols), right_her...]
    all_to_all x1 -> x0, waiting for transfers between devices: 15.1 us -> none  [on_device(): lax.all_to_all(lax.all_to_all(product, 'col', split_axis=2, concat_axis=0...]
    all_gather x1 -> x0, local copies, waits for them, and re-layouts: 9.14 us -> none  [on_device(): lax.all_gather(right_proj, ('row', 'seq'), axis=0, tiled=True)]
    all_to_all x1 -> x0, starting transfers between devices: 8.44 us -> none  [on_device(): lax.all_to_all(lax.all_to_all(product, 'col', split_axis=2, concat_axis=0...]
  transfers between devices with their start and end apart: 5 -> 0, of which waited for: 5 -> 0; matrix products, arithmetic and copies ran while one was open for 2% -> 0% of each run, Pallas kernels for 0% -> 0%
where the time goes in v1:
time: 150 us; the launch traced here: 149 us
  Pallas kernels  133 us (89%)
  local copies, waits for them, and re-layouts  8.93 us (6%)
  matrix products  5.35 us (4%)
  other arithmetic  2.17 us (1%)
    pallas_call x1, Pallas kernels, spread_triangle(): pl.pallas_call(spread_kernel, out_shape=(jax.ShapeDtypeStruct((NX, NZ, NS...  50.1 us
    pallas_call x1, Pallas kernels, gather_factors(): pl.pallas_call(gather_kernel, out_shape=(jax.ShapeDtypeStruct((NZ, NY, 2,...  39.3 us
    pallas_call x1, Pallas kernels, return_product(): pl.pallas_call(return_kernel, out_shape=(out, out), in_specs=[VMEM, VMEM]...  24.6 us
    pallas_call x1, Pallas kernels, outer_and_gates(): pl.pallas_call(functools.partial(outer_kernel, depth // factor), out_shap...  14.9 us
    unnamed x27, local copies, waits for them, and re-layouts  5.96 us
    pallas_call x1, Pallas kernels, final_update(): pl.pallas_call(final_kernel, out_shape=jax.ShapeDtypeStruct((rows, cols,...  3.51 us

profile of v1, /device:TPU:1, one launch (start us, length us, event | category | flops | bytes accessed | tf_op | source)
XLA Modules:
  0.0 149.2 jit_solution(8911649395936093951)
XLA Ops:
  0.0 0.0 copy-start
  0.0 0.0 copy-start.10
  0.0 0.0 copy-start.9
  0.0 0.0 copy-start.8
  0.0 0.0 copy-start.7
  0.0 0.0 copy-start.4
  0.0 1.1 convert_reduce_fusion
  1.1 1.1 fusion.5
  2.2 0.0 copy-done
  2.2 1.2 convolution_convert_fusion
  3.4 1.8 %fusion.1.right_ref = bf16[32,256]{1,0:T(8,128)(2,1)} fusion(bf16[256,32]{0,1:T(8,128)(2,1)} %param.14, bf16[1,256,256]{2,1,0:T(8,128)(2,1)} %param.12, f32[256]{0:T(256)S(1)} %add_rsqrt_fusion, f32[256]{0:T(256)S(1)} %broadcast_multiply_fusion), kind=kOutput, calls=%fused_computation.4 | convolution fusion | flops 4464640 | bytes 165888 | tf_op jit(solution)/shard_map/dot_general | solution.py:518
  5.2 0.1 copy.18
  5.3 0.7 reshape.52.left_ref
  6.0 1.1 copy.20
  7.1 0.1 copy.21.out_ref
  7.2 39.3 %gather_factors.1 = (bf16[8,8,2,32,256]{4,3,2,1,0:T(8,128)(2,1)}, bf16[8,16,2,128]{3,2,1,0:T(2,128)(2,1)}) custom-call(bf16[32,256]{1,0:T(8,128)(2,1)} %fusion.1.right_ref, bf16[2,16,2,128]{3,2,1,0:T(2,128)(2,1)} %reshape.52.left_ref), custom_call_target="tpu_custom_call" | custom-call | tf_op jit(solution)/shard_map/gather_factors/pallas_call | solution.py:182
  46.6 0.9 copy.24
  47.4 0.1 copy.19
  47.5 0.0 copy-done.10
  47.6 0.0 copy-done.9
  47.6 0.0 copy-done.8
  47.6 0.0 copy-done.7
  47.6 0.0 copy-done.4
  47.6 0.0 copy-start.1
  47.6 1.6 %copy-done.1 = bf16[8,8,2,32,256]{4,3,2,1,0:T(8,128)(2,1)S(1)} copy-done((bf16[8,8,2,32,256]{4,3,2,1,0:T(8,128)(2,1)S(1)}, bf16[8,8,2,32,256]{4,3,2,1,0:T(8,128)(2,1)}, u32[]{:S(2)}) %copy-start.1) | copy-done | bytes 2097176
  49.2 14.9 %outer_and_gates.1 = (bf16[128,8,256]{2,1,0:T(8,128)(2,1)S(1)}, bf16[128,8,256]{2,1,0:T(8,128)(2,1)S(1)}, bf16[8,128,256]{2,1,0:T(8,128)(2,1)S(1)}, bf16[8,128,256]{2,1,0:T(8,128)(2,1)S(1)}) custom-call(bf16[256,128]{1,0:T(8,128)(2,1)S(1)} %bitcast.48, bf16[4096,256]{1,0:T(8,128)(2,1)S(1)} %bitcast.43, bf16[128,1024]{1,0:T(8,128)(2,1)S(1)} %copy.21.out_ref, ...), custom_call_target="tpu_custom_call" | custom-call | tf_op jit(solution)/shard_map/outer_and_gates/pallas_call | solution.py:450
  64.1 0.0 copy-start.2
  64.1 0.8 copy-done.2
  64.9 0.0 copy-start.3
  64.9 0.8 copy-done.3
  65.7 50.1 %spread_triangle.1 = (bf16[4,8,16,8,256]{4,3,2,1,0:T(8,128)(2,1)}, bf16[4,2,16,8,256]{4,3,2,1,0:T(8,128)(2,1)}) custom-call(bf16[8,16,8,256]{3,2,1,0:T(8,128)(2,1)} %bitcast.44, bf16[8,16,8,256]{3,2,1,0:T(8,128)(2,1)} %bitcast.45), custom_call_target="tpu_custom_call" | custom-call | tf_op jit(solution)/shard_map/spread_triangle/pallas_call | solution.py:301
  115.9 0.0 copy-start.11
  115.9 0.0 copy-start.12
  115.9 2.4 %fusion = bf16[1024,256]{1,0:T(8,128)(2,1)S(1)} fusion(bf16[4,1024,256]{2,1,0:T(8,128)(2,1)} %bitcast.55, bf16[4,256,256]{2,1,0:T(8,128)(2,1)} %bitcast.56), kind=kOutput, calls=%fused_computation.1 | convolution fusion | flops 537133056 | bytes 3145728 | tf_op jit(solution)/shard_map/xik,xjk->ij/dot_general | solution.py:537
  118.3 0.8 fusion.9
  119.1 24.6 %return_product.1 = (bf16[8,16,8,128]{3,2,1,0:T(8,128)(2,1)}, bf16[8,16,8,128]{3,2,1,0:T(8,128)(2,1)}) custom-call(bf16[8,16,8,128]{3,2,1,0:T(8,128)(2,1)} %bitcast.51, bf16[8,16,8,128]{3,2,1,0:T(8,128)(2,1)} %bitcast.50), custom_call_target="tpu_custom_call" | custom-call | tf_op jit(solution)/shard_map/return_product/pallas_call | solution.py:351
  143.8 0.0 copy-done.11
  143.8 0.0 copy-done.12
  143.8 0.0 copy-start.5
  143.8 0.9 copy-done.5
  144.8 0.0 copy-start.6
  144.8 0.9 copy-done.6
  145.7 3.5 %final_update.1 = bf16[8,256,128]{2,1,0:T(8,128)(2,1)} custom-call(bf16[128,8,128]{2,1,0:T(8,128)(2,1)S(1)} %bitcast.46, bf16[128,8,128]{2,1,0:T(8,128)(2,1)S(1)} %bitcast.47, bf16[8,128,256]{2,1,0:T(8,128)(2,1)S(1)} %get-tuple-element.23.mid_ref, bf16[8,128,256]{2,1,0:T(8,128)(2,1)S(1)} %get-tuple-element.24.normed_ref, bf16[128,128]{1,0:T(8,128)(2,1)S(1)} %copy-done.11, ...), custom_call_target="tpu_custom_call" | custom-call | tf_op jit(solution)/shard_map/final_update/pallas_call | solution.py:487
  (2 shorter events, 0.0 us)
Async XLA Ops:
  0.0 2.2 %copy-start = (bf16[256,32]{0,1:T(8,128)(2,1)S(1)}, bf16[256,32]{0,1:T(8,128)(2,1)}, u32[]{:S(2)}) copy-start(bf16[256,32]{0,1:T(8,128)(2,1)} %param.13) | copy-start | bytes 49156
  0.0 47.5 %copy-start.10 = (bf16[128,128]{1,0:T(8,128)(2,1)S(1)}, bf16[128,128]{1,0:T(8,128)(2,1)}, u32[]{:S(2)}) copy-start(bf16[128,128]{1,0:T(8,128)(2,1)} %wrg_ref.1) | copy-start | bytes 98308
  0.0 47.5 %copy-start.9 = (bf16[128,128]{1,0:T(8,128)(2,1)S(1)}, bf16[128,128]{1,0:T(8,128)(2,1)}, u32[]{:S(2)}) copy-start(bf16[128,128]{1,0:T(8,128)(2,1)} %wr_ref.1) | copy-start | bytes 98308
  0.0 47.6 %copy-start.8 = (bf16[128,128]{1,0:T(8,128)(2,1)S(1)}, bf16[128,128]{1,0:T(8,128)(2,1)}, u32[]{:S(2)}) copy-start(bf16[128,128]{1,0:T(8,128)(2,1)} %wlg_ref.1) | copy-start | bytes 98308
  0.0 47.6 %copy-start.7 = (bf16[128,128]{1,0:T(8,128)(2,1)S(1)}, bf16[128,128]{1,0:T(8,128)(2,1)}, u32[]{:S(2)}) copy-start(bf16[128,128]{1,0:T(8,128)(2,1)} %wl_ref.1) | copy-start | bytes 98308
  0.0 47.6 %copy-start.4 = (bf16[8,256,128]{2,1,0:T(8,128)(2,1)S(1)}, bf16[8,256,128]{2,1,0:T(8,128)(2,1)}, u32[]{:S(2)}) copy-start(bf16[8,256,128]{2,1,0:T(8,128)(2,1)} %pair_ref.1) | copy-start | bytes 1572868
  47.6 1.6 %copy-start.1 = (bf16[8,8,2,32,256]{4,3,2,1,0:T(8,128)(2,1)S(1)}, bf16[8,8,2,32,256]{4,3,2,1,0:T(8,128)(2,1)}, u32[]{:S(2)}) copy-start(bf16[8,8,2,32,256]{4,3,2,1,0:T(8,128)(2,1)} %get-tuple-element.16) | copy-start | bytes 6291460
  64.1 0.8 copy-start.2
  64.9 0.8 copy-start.3
  115.9 27.9 %copy-start.11 = (bf16[128,128]{1,0:T(8,128)(2,1)S(1)}, bf16[128,128]{1,0:T(8,128)(2,1)}, u32[]{:S(2)}) copy-start(bf16[128,128]{1,0:T(8,128)(2,1)} %gate_ref.1) | copy-start | bytes 98308
  115.9 27.9 %copy-start.12 = (bf16[128,128]{1,0:T(8,128)(2,1)S(1)}, bf16[128,128]{1,0:T(8,128)(2,1)}, u32[]{:S(2)}) copy-start(bf16[128,128]{1,0:T(8,128)(2,1)} %out_w_ref.1) | copy-start | bytes 98308
  143.8 1.0 copy-start.5
  144.8 0.9 copy-start.6

commit v2 on v0

v2 whole, which is shorter than its diff:
```python
import jax
import jax.numpy as jnp
from jax import lax
from jax.experimental import pallas as pl
from jax.experimental.pallas import tpu as pltpu
from jax.sharding import PartitionSpec as P

EPS = 1e-05
MESH = pl.DeviceIdType.MESH
F32 = jnp.float32
BF16 = jnp.bfloat16
VMEM = pl.BlockSpec(memory_space=pltpu.VMEM)
ANY = pl.BlockSpec(memory_space=pl.ANY)
DMA = pltpu.SemaphoreType.DMA

NX = 4
NZ = 8
NQ = 8
NS = 2 * NQ
NY = NS // 2
HOPS = (1, 7, 2, 6, 3, 5, 4)


class Place:
    def __init__(self):
        row = lax.axis_index("row")
        self.x = lax.axis_index("col")
        seq = lax.axis_index("seq")
        self.z = row // 2
        self.s = (row % 2) * NQ + seq
        self.yy = self.s // 2
        self.core = self.s % 2

    def at(self, z=None, s=None, x=None):
        z = self.z if z is None else z
        s = self.s if s is None else s
        x = self.x if x is None else x
        return (z * 2 + s // NQ, x, s % NQ)


def send(src, dst, send_sem, recv_sem, device):
    pltpu.make_async_remote_copy(
        src_ref=src,
        dst_ref=dst,
        send_sem=send_sem,
        recv_sem=recv_sem,
        device_id=device,
        device_id_type=MESH,
    ).start()


def keep(src, dst, sem):
    pltpu.make_async_copy(src, dst, sem).start()


def await_bytes(ref, sem):
    pltpu.make_async_copy(ref, ref, sem).wait()


def greet(device):
    pl.semaphore_signal(
        pltpu.get_barrier_semaphore(), inc=1, device_id=device, device_id_type=MESH
    )


def layer_norm(values, axis):
    values = values.astype(F32)
    center = values - jnp.mean(values, axis=axis, keepdims=True)
    spread = jnp.mean(center * center, axis=axis, keepdims=True)
    return center * lax.rsqrt(spread + EPS)


def turned(ref):
    return ref[...].astype(F32).T.astype(BF16)


def dot(a, b):
    return jnp.dot(a, b, preferred_element_type=F32)


def lanes(h):
    return slice(h * 128, (h + 1) * 128)


def flat_rows(ref):
    values = ref[...].astype(F32)
    return values.reshape(-1, values.shape[-1]).astype(BF16)


def split_rows(values):
    return values.reshape(-1, 8, values.shape[-1]).astype(BF16)


def factors(align_ref, wl_ref, wr_ref, normed, left_own, right_own):
    cols, width = align_ref.shape[1:]
    p = wl_ref.shape[1]
    seq = layer_norm(align_ref[0], 1).astype(BF16)
    right_own[...] = lax.dot_general(
        turned(wr_ref), seq, (((1,), (1,)), ((), ())), preferred_element_type=F32
    ).astype(BF16)
    wide = seq.astype(F32)
    for h in range(width // 128):
        normed[h] = wide[:, lanes(h)]
    lane = lax.broadcasted_iota(jnp.int32, (p, 8 * p), 1)
    unit = lax.broadcasted_iota(jnp.int32, (p, 8 * p), 0)
    tile = jnp.where(lane % p == unit, 1.0, 0.0).astype(BF16)
    repeated = dot(wl_ref[...], tile)
    group = lax.broadcasted_iota(jnp.int32, repeated.shape, 1) // p
    total = None
    for i in range(8):
        rows = jnp.concatenate(
            [normed[h, pl.ds(i, cols // 8, stride=8), :] for h in range(width // 128)], axis=1
        ).astype(BF16)
        term = dot(rows, jnp.where(group == i, repeated, 0.0).astype(BF16))
        total = term if total is None else total + term
    left_own[...] = total.astype(BF16).reshape(left_own.shape)


def greet_all(me):
    for t in range(1, NS):
        greet(me.at(s=(me.s + t) % NS))
    for t in range(1, NZ):
        greet(me.at(z=(me.z + t) % NZ))
    for t in range(1, NX):
        greet(me.at(x=(me.x + t) % NX))
    owner = me.z // 2
    for t in range(NZ):

        @pl.when(jnp.logical_not(jnp.logical_and(owner == me.x, me.z == t)))
        def _():
            greet(me.at(z=t, x=owner))

    return NS - 1 + NZ - 1 + NX - 1 + 8 - jnp.where(owner == me.x, 1, 0)


def gather(me, left_own, right_own, half, half_wide, mine_send, mine, every, wide, prepare, sems):
    send_sem, first_sem, next_sem, twin_sem, left_sem = sems
    z, s, x, yy, core = me.z, me.s, me.x, me.yy, me.core
    q = right_own.shape[0]
    here = jnp.where(z // 2 == x, 1, 0)

    own = every.at[z, yy, core]
    keep(right_own, own, first_sem)

    @pl.when(core == 0)
    def _():
        for t in HOPS:
            send(right_own, own, send_sem.at[1], first_sem, me.at(z=(z + t) % NZ))

    @pl.when(core == 1)
    def _():
        for t in HOPS:
            send(right_own, own, send_sem.at[1], first_sem, me.at(s=(s + 2 * t) % NS))

    for h in range(2):
        for xt in range(NX):
            zt = 2 * x + h
            same = jnp.logical_and(x == xt, z == zt)

            @pl.when(same)
            def _():
                keep(left_own.at[h], half.at[z], left_sem.at[0])

            @pl.when(jnp.logical_not(same))
            def _():
                send(left_own.at[h], half.at[z], send_sem.at[0], left_sem.at[0], me.at(z=zt, x=xt))

    await_bytes(every.at[:, 0, 0], first_sem)
    twin = me.at(s=s + 1 - 2 * core)

    @pl.when(core == 0)
    def _():
        line = every.at[:, yy, 0]
        for t in HOPS:
            send(line, line, send_sem.at[3], next_sem.at[yy], me.at(s=(s + 2 * t) % NS))
        send(line, line, send_sem.at[4], twin_sem.at[yy], twin)

    @pl.when(core == 1)
    def _():
        line = every.at[z, :, 1]
        for t in HOPS:
            send(line, line, send_sem.at[3], next_sem.at[z], me.at(z=(z + t) % NZ))
        send(line, line, send_sem.at[4], twin_sem.at[z], twin)

    await_bytes(half, left_sem.at[0])
    for h in range(2):
        half_wide[h] = half[:, :, lanes(h)].astype(F32).reshape(NZ * NS, 128)
    for b in range(NS):
        mine_send[b] = jnp.concatenate(
            [half_wide[h, pl.ds(b, NZ, stride=NS), :] for h in range(2)], axis=1
        ).astype(BF16)
    prepare()
    keep(mine_send.at[s], mine.at[s], left_sem.at[1])
    for t in range(1, NS):
        st = (s + t) % NS
        send(mine_send.at[st], mine.at[s], send_sem.at[2], left_sem.at[1], me.at(s=st))

    @pl.when(core == 0)
    def _():
        for t in HOPS:
            yt = (yy + t) % NY
            part = every.at[:, yt, 0]
            await_bytes(part, next_sem.at[yt])
            send(part, part, send_sem.at[4], twin_sem.at[yt], twin)

    @pl.when(core == 1)
    def _():
        for t in HOPS:
            zt = (z + t) % NZ
            part = every.at[zt, :, 1]
            await_bytes(part, next_sem.at[zt])
            send(part, part, send_sem.at[4], twin_sem.at[zt], twin)

    await_bytes(mine, left_sem.at[1])
    for t in range(8):
        await_bytes(every.at[:, 0, 0], twin_sem.at[t])

    @pl.loop(0, NZ * NY)
    def _(k):
        at = pl.ds(pl.multiple_of(k * 2 * q, 2 * q), 2 * q)
        block = every[k // NY, k % NY].astype(F32).reshape(2 * q, -1)
        for h in range(2):
            wide[h, at, :] = block[:, lanes(h)]

    @pl.when(here == 1)
    def _():
        await_bytes(half.at[pl.ds(0, 7)], send_sem.at[0])

    @pl.when(here == 0)
    def _():
        await_bytes(half, send_sem.at[0])

    await_bytes(every.at[pl.ds(0, 7), 0, 0], send_sem.at[1])
    await_bytes(mine.at[pl.ds(0, NS - 1)], send_sem.at[2])
    await_bytes(every.at[pl.ds(0, 7), :, 0], send_sem.at[3])
    await_bytes(every.at[:, :, 0], send_sem.at[4])


def outer_and_gates(mine, mine_wide, wide, out_w, pair, weights, stack, mid_all, normed_all, acc, sides):
    rows, cols, width = pair.shape
    factor = mine.shape[2] // rows
    seqs = NZ * NS
    for h in range(2):
        mine_wide[h] = mine[:, :, lanes(h)].astype(F32).reshape(seqs, 128)
    left = jnp.concatenate(
        [
            jnp.concatenate(
                [mine_wide[h, pl.ds(z, NS, stride=NZ), :] for z in range(NZ)], axis=0
            ).T
            for h in range(2)
        ],
        axis=0,
    ).astype(BF16)

    @pl.loop(0, factor)
    def _(q):
        part = jnp.concatenate(
            [wide[h, pl.ds(q, seqs, stride=factor), :] for h in range(2)], axis=1
        ).astype(BF16)
        outer = dot(left, part) * (1.0 / seqs)
        at = pl.ds(pl.multiple_of(q * factor, factor), factor)
        stack[:, at, :] = outer.astype(BF16).reshape(rows, factor, cols)

    wl, wlg, wr, wrg = (turned(ref) for ref in weights)
    hidden = wl.shape[0]

    @pl.loop(0, rows)
    def _(i):
        mid = (dot(out_w[...], stack[i]) + pair[i].astype(F32).T).astype(BF16)
        mid_all[i] = mid
        normed = layer_norm(mid, 0).astype(BF16)
        normed_all[i] = normed
        for k, (gate, value) in enumerate(((wlg, wl), (wrg, wr))):
            side = jax.nn.sigmoid(dot(gate, normed)) * dot(value, normed)
            for h in range(2):
                acc[k, h, pl.ds(i, hidden, stride=rows), :] = side[:, lanes(h)]

    for k in range(2):
        for h in range(2):
            sides[k][:, :, :, lanes(h)] = split_rows(acc[k, h]).reshape(NZ, NS, rows, 128)


def first_legs(me, a_in, b_in, a_mid, b_mid, send_sem, a_sem, b_sem):
    z, s = me.z, me.s
    keep(a_in.at[:, s], a_mid.at[s], a_sem)
    keep(b_in.at[z], b_mid.at[z], b_sem)
    for t in range(1, NS):
        st = (s + t) % NS
        send(a_in.at[:, st], a_mid.at[s], send_sem.at[0], a_sem, me.at(s=st))
        if t <= len(HOPS):
            zt = (z + HOPS[t - 1]) % NZ
            send(b_in.at[zt], b_mid.at[z], send_sem.at[1], b_sem, me.at(z=zt))


def sent_legs(a_mid, b_mid, send_sem):
    await_bytes(a_mid.at[pl.ds(0, NS - 1)], send_sem.at[0])
    await_bytes(b_mid.at[pl.ds(0, NZ - 1)], send_sem.at[1])
    await_bytes(a_mid.at[:, pl.ds(0, NZ - 1)], send_sem.at[2])
    await_bytes(b_mid.at[:, pl.ds(0, NS - 1)], send_sem.at[3])


def spread(me, a_in, b_in, a_out, b_out, a_mid, b_mid, b_all, sems):
    send_sem, first_sem, a_sem, b_sem, right_sem, left_sem, far_sem, side_sem = sems
    z, s, x = me.z, me.s, me.x
    first_legs(me, a_in, b_in, a_mid, b_mid, send_sem, first_sem.at[0], first_sem.at[1])
    await_bytes(a_mid, first_sem.at[0])
    keep(a_mid.at[:, z], a_out.at[x, z], a_sem.at[z])
    for t in HOPS:
        zt = (z + t) % NZ
        send(a_mid.at[:, zt], a_out.at[x, z], send_sem.at[2], a_sem.at[z], me.at(z=zt))
    await_bytes(b_mid, first_sem.at[1])
    keep(b_mid.at[:, s], b_all.at[:, s], b_sem)
    for t in range(1, NS):
        st = (s + t) % NS
        send(b_mid.at[:, st], b_all.at[:, s], send_sem.at[3], b_sem, me.at(s=st))

    after, before = (x + 1) % NX, (x + 3) % NX

    def pass_on(t):
        zt = (z + t) % NZ
        if t in (0, 5, 6, 7):
            part = a_out.at[before, zt]
            await_bytes(part, left_sem.at[zt])
            send(part, part, send_sem.at[5], far_sem.at[zt], me.at(x=after))
        else:
            part = a_out.at[after, zt]
            await_bytes(part, right_sem.at[zt])
            send(part, part, send_sem.at[5], far_sem.at[zt], me.at(x=before))

    order = (0,) + HOPS
    for k, t in enumerate(order):
        zt = (z + t) % NZ
        part = a_out.at[x, zt]
        await_bytes(part, a_sem.at[zt])
        send(part, part, send_sem.at[4], left_sem.at[zt], me.at(x=after))
        send(part, part, send_sem.at[4], right_sem.at[zt], me.at(x=before))
        if k >= 2:
            pass_on(order[k - 2])
    await_bytes(b_all, b_sem)
    keep(b_all.at[pl.ds(2 * x, 2)], b_out.at[x], side_sem)
    for t in range(1, NX):
        xt = (x + t) % NX
        send(b_all.at[pl.ds(2 * xt, 2)], b_out.at[x], send_sem.at[6], side_sem, me.at(x=xt))
    for t in order[-2:]:
        pass_on(t)
    await_bytes(b_out, side_sem)


def multiply(me, a_out, b_out, product, cols_all, sems):
    right_sem, left_sem, far_sem = sems
    order = (0,) + HOPS
    rows = b_out.shape[1] * b_out.shape[2] * b_out.shape[3]
    for k in range(NX):
        cols_all[k] = flat_rows(b_out.at[k])
    for t in order:
        zt = (me.z + t) % NZ
        part = a_out.at[me.x, zt]
        await_bytes(part, far_sem.at[zt])
        await_bytes(part, (right_sem if t in (0, 5, 6, 7) else left_sem).at[zt])
        total = None
        for k in range(NX):
            term = lax.dot_general(
                flat_rows(a_out.at[k, zt]),
                cols_all[k],
                (((1,), (1,)), ((), ())),
                preferred_element_type=F32,
            )
            total = term if total is None else total + term
        for h in range(2):
            product[h][zt] = split_rows(total[:, lanes(h)])


def bring_back(me, a_in, b_in, a_out, b_out, a_mid, b_mid, sems):
    send_sem, first_sem, last_sem = sems
    z, s = me.z, me.s
    first_legs(me, a_in, b_in, a_mid, b_mid, send_sem, first_sem.at[0], first_sem.at[1])
    await_bytes(a_mid, first_sem.at[0])
    keep(a_mid.at[:, z], a_out.at[z], last_sem.at[0])
    for t in HOPS:
        zt = (z + t) % NZ
        send(a_mid.at[:, zt], a_out.at[z], send_sem.at[2], last_sem.at[0], me.at(z=zt))
    await_bytes(b_mid, first_sem.at[1])
    keep(b_mid.at[:, s], b_out.at[:, s], last_sem.at[1])
    for t in range(1, NS):
        st = (s + t) % NS
        send(b_mid.at[:, st], b_out.at[:, s], send_sem.at[3], last_sem.at[1], me.at(s=st))
    await_bytes(a_out, last_sem.at[0])
    await_bytes(b_out, last_sem.at[1])


def finish(parts, wide, mid_all, normed_all, gate_ref, out_ref, result):
    rows, width, cols = mid_all.shape
    for h, ref in enumerate(parts):
        wide[h] = ref[...].astype(F32).reshape(-1, 128)
    hidden = wide.shape[1] // rows
    gate_w, out_w = turned(gate_ref), turned(out_ref)

    @pl.loop(0, rows)
    def _(i):
        product = jnp.concatenate(
            [wide[h, pl.ds(i, hidden, stride=rows), :] for h in range(2)], axis=1
        )
        normed = layer_norm(product, 0).astype(BF16)
        gate = jax.nn.sigmoid(dot(gate_w, normed_all[i]))
        result[i] = (mid_all[i].astype(F32) + gate * dot(out_w, normed)).T.astype(BF16)


def kernel(
    pair_hbm,
    opm_out_hbm,
    align_ref,
    opm_left_ref,
    opm_right_ref,
    tri_left_ref,
    tri_left_gate_ref,
    tri_right_ref,
    tri_right_gate_ref,
    tri_gate_ref,
    tri_out_ref,
    result,
    pair,
    opm_out,
    opm_wide,
    out_w,
    normed_seq,
    left_own,
    right_own,
    half,
    half_wide,
    mine_send,
    mine,
    every,
    wide,
    stack,
    mid_all,
    normed_all,
    acc,
    left_side,
    right_side,
    a_mid,
    b_mid,
    b_all,
    a_out,
    b_out,
    cols_all,
    product_a,
    product_b,
    pa_mid,
    pb_mid,
    pa_out,
    pb_out,
    load_sem,
    g_send,
    g_first,
    g_next,
    g_twin,
    g_left,
    s_send,
    s_first,
    s_a,
    s_b,
    s_right,
    s_left,
    s_far,
    s_side,
    r_send,
    r_first,
    r_last,
):
    me = Place()
    count = greet_all(me)
    keep(pair_hbm, pair, load_sem.at[0])
    keep(opm_out_hbm, opm_out, load_sem.at[1])
    factors(align_ref, opm_left_ref, opm_right_ref, normed_seq, left_own, right_own)
    pl.semaphore_wait(pltpu.get_barrier_semaphore(), count)

    def prepare():
        await_bytes(opm_out, load_sem.at[1])
        await_bytes(pair, load_sem.at[0])
        opm_wide[...] = opm_out[...].astype(F32)
        p = opm_left_ref.shape[1]
        q = opm_right_ref.shape[1]
        for k in range(q):
            rows = opm_wide[pl.ds(k, p, stride=q), :]
            mine_rows = slice(k * p, (k + 1) * p)
            stack[0, mine_rows, 0:128] = rows.astype(BF16)
        out_w[...] = stack[0, :, 0:128].astype(F32).T.astype(BF16)

    gather(
        me,
        left_own,
        right_own,
        half,
        half_wide,
        mine_send,
        mine,
        every,
        wide,
        prepare,
        (g_send, g_first, g_next, g_twin, g_left),
    )
    outer_and_gates(
        mine,
        half_wide,
        wide,
        out_w,
        pair,
        (tri_left_ref, tri_left_gate_ref, tri_right_ref, tri_right_gate_ref),
        stack,
        mid_all,
        normed_all,
        acc,
        (left_side, right_side),
    )
    spread(
        me,
        left_side,
        right_side,
        a_out,
        b_out,
        a_mid,
        b_mid,
        b_all,
        (s_send, s_first, s_a, s_b, s_right, s_left, s_far, s_side),
    )
    multiply(me, a_out, b_out, (product_a, product_b), cols_all, (s_right, s_left, s_far))
    bring_back(
        me, product_a, product_b, pa_out, pb_out, pa_mid, pb_mid, (r_send, r_first, r_last)
    )
    finish((pa_out, pb_out), acc.at[0], mid_all, normed_all, tri_gate_ref, tri_out_ref, result)

    sent_legs(a_mid, b_mid, s_send)
    await_bytes(a_out.at[pl.ds(0, 2)], s_send.at[4])
    await_bytes(a_out.at[0], s_send.at[5])
    await_bytes(b_out.at[pl.ds(0, NX - 1)], s_send.at[6])
    sent_legs(pa_mid, pb_mid, r_send)


def on_device(pair, alignment, opm_left, opm_right, opm_out, *weights):
    rows, cols, width = pair.shape
    model = alignment.shape[2]
    factor = opm_left.shape[1]
    hidden = weights[0].shape[1]
    seqs = NZ * NS

    def vb(*shape):
        return pltpu.VMEM(shape, BF16)

    def vf(*shape):
        return pltpu.VMEM(shape, F32)

    scratch = [
        vb(rows, cols, width),
        vb(factor * factor, width),
        vf(factor * factor, width),
        vb(width, factor * factor),
        vf(model // 128, cols, 128),
        vb(2, NS, rows * factor),
        vb(factor, cols),
        vb(NZ, NS, rows * factor),
        vf(2, seqs, 128),
        vb(NS, NZ, rows * factor),
        vb(NS, NZ, rows * factor),
        vb(NZ, NY, 2, factor, cols),
        vf(2, seqs * factor, 128),
        vb(rows, factor * factor, cols),
        vb(rows, width, cols),
        vb(rows, width, cols),
        vf(2, 2, hidden * rows, 128),
        vb(NZ, NS, rows, cols),
        vb(NZ, NS, rows, cols),
        vb(NS, NZ, rows, cols),
        vb(NZ, NS, rows, cols),
        vb(NZ, NS, rows, cols),
        vb(NX, NZ, NS, rows, cols),
        vb(NX, NZ // NX, NS, rows, cols),
        vb(NX, cols, cols),
        vb(NZ, NS, rows, 128),
        vb(NZ, NS, rows, 128),
        vb(NS, NZ, rows, 128),
        vb(NZ, NS, rows, 128),
        vb(NZ, NS, rows, 128),
        vb(NZ, NS, rows, 128),
        DMA((2,)),
        DMA((5,)),
        DMA,
        DMA((8,)),
        DMA((8,)),
        DMA((2,)),
        DMA((7,)),
        DMA((2,)),
        DMA((NZ,)),
        DMA,
        DMA((NZ,)),
        DMA((NZ,)),
        DMA((NZ,)),
        DMA,
        DMA((4,)),
        DMA((2,)),
        DMA((2,)),
    ]
    return pl.pallas_call(
        kernel,
        out_shape=jax.ShapeDtypeStruct((rows, cols, width), BF16),
        in_specs=[ANY, ANY] + [VMEM] * 9,
        out_specs=VMEM,
        scratch_shapes=scratch,
        compiler_params=pltpu.CompilerParams(
            collective_id=0, has_side_effects=True, vmem_limit_bytes=56 << 20
        ),
        name="evoformer_pair",
    )(pair, opm_out, alignment, opm_left, opm_right, *weights)


def solution(mesh):
    split = P(("row", "seq"), "col", None)
    return jax.shard_map(
        on_device,
        mesh=mesh,
        in_specs=(split, split) + (P(),) * 9,
        out_specs=split,
        check_vma=False,
    )
```

time: 819 us -> 127 us (0.16)
  waiting for transfers between devices: 651 us -> 0 us
  Pallas kernels: 0 us -> 122 us
  blocking collectives: 86.2 us -> 0 us
  matrix products: 29.9 us -> 0 us
  local copies, waits for them, and re-layouts: 23.1 us -> 4.08 us
  between operations: 13.5 us -> 0.01 us
  starting transfers between devices: 8.57 us -> 0 us
    all_gather x3 -> x0, waiting for transfers between devices: 597 us -> none  [the longest x1 223 us: on_device(): lax.all_gather(left_proj, ('row', 'seq'), axis=0, tiled=True)]
    pallas_call x0 -> x1, Pallas kernels: none -> 122 us  [on_device(): pl.pallas_call(kernel, out_shape=jax.ShapeDtypeStruct((rows, cols, width)...]
    all_to_all x5 -> x0, blocking collectives: 86.2 us -> none  [the longest x1 27.8 us: on_device(): lax.all_to_all(lax.all_to_all(left_first, 'col', split_axis=0, concat_axi...]
    psum x1 -> x0, waiting for transfers between devices: 38.8 us -> none  [spread_2(): return lax.psum(jnp.where(mine, shard, jnp.zeros_like(shard)), axis)]
    dot_general x25 -> x0, matrix products: 29.9 us -> none  [the longest x8 9.69 us: outer_row(): jnp.dot(mean_outer, opm_out, preferred_element_type=jnp.float32)]
    all_to_all x1 -> x0, waiting for transfers between devices: 15.1 us -> none  [on_device(): lax.all_to_all(lax.all_to_all(product, 'col', split_axis=2, concat_axis=0...]
    all_gather x1 -> x0, local copies, waits for them, and re-layouts: 9.14 us -> none  [on_device(): lax.all_gather(right_proj, ('row', 'seq'), axis=0, tiled=True)]
    all_to_all x1 -> x0, starting transfers between devices: 8.44 us -> none  [on_device(): lax.all_to_all(lax.all_to_all(product, 'col', split_axis=2, concat_axis=0...]
  transfers between devices with their start and end apart: 5 -> 0, of which waited for: 5 -> 0; matrix products, arithmetic and copies ran while one was open for 2% -> 0% of each run, Pallas kernels for 0% -> 0%
where the time goes in v2:
time: 127 us; the launch traced here: 126 us
  Pallas kernels  122 us (96%)
  local copies, waits for them, and re-layouts  4.08 us (3%)
    pallas_call x1, Pallas kernels, on_device(): pl.pallas_call(kernel, out_shape=jax.ShapeDtypeStruct((rows, cols, width)...  122 us
    unnamed x5, local copies, waits for them, and re-layouts  4.08 us

profile of v2, /device:TPU:1, one launch (start us, length us, event | category | flops | bytes accessed | tf_op | source)
XLA Modules:
  0.0 125.9 jit_solution(6169172443977201329)
XLA Ops:
  0.0 0.0 copy-start
  0.0 1.5 %copy.12.opm_left_ref = bf16[256,32]{1,0:T(8,128)(2,1)} copy(bf16[256,32]{0,1:T(8,128)(2,1)} %param.13) | data formatting | bytes 32768 | tf_op args[2]
  1.5 0.0 copy-done
  1.5 0.7 copy.13.opm_right_ref
  2.2 121.8 %evoformer_pair.1 = bf16[8,256,128]{2,1,0:T(8,128)(2,1)} custom-call(bf16[8,256,128]{2,1,0:T(8,128)(2,1)} %pair_hbm.1, bf16[1024,128]{1,0:T(8,128)(2,1)} %opm_out_hbm.1, bf16[1,256,256]{2,1,0:T(8,128)(2,1)} %align_ref.1, bf16[256,32]{1,0:T(8,128)(2,1)} %copy.12.opm_left_ref, bf16[256,32]{1,0:T(8,128)(2,1)} %copy.13.opm_right_ref, ...), custom_call_target="tpu_custom_call" | custom-call | tf_op jit(solution)/shard_map/evoformer_pair/pallas_call | solution.py:602
  124.0 1.9 %copy.15 = bf16[8,256,128]{2,1,0:T(8,128)(2,1)} copy(bf16[8,256,128]{2,1,0:T(8,128)(2,1)} %evoformer_pair.1) | data formatting | bytes 1048576
Async XLA Ops:
  0.0 1.5 %copy-start = (bf16[256,32]{0,1:T(8,128)(2,1)S(1)}, bf16[256,32]{0,1:T(8,128)(2,1)}, u32[]{:S(2)}) copy-start(bf16[256,32]{0,1:T(8,128)(2,1)} %param.14) | copy-start | bytes 49156

commit v3 on v2

--- a/solution.py
+++ b/solution.py
@@ -93,10 +93,10 @@
 
 def factors(align_ref, wl_ref, wr_ref, normed, left_own, right_own):
     cols, width = align_ref.shape[1:]
-    p = wl_ref.shape[1]
+    p = wl_ref.shape[0]
     seq = layer_norm(align_ref[0], 1).astype(BF16)
     right_own[...] = lax.dot_general(
-        turned(wr_ref), seq, (((1,), (1,)), ((), ())), preferred_element_type=F32
+        wr_ref[...], seq, (((1,), (1,)), ((), ())), preferred_element_type=F32
     ).astype(BF16)
     wide = seq.astype(F32)
     for h in range(width // 128):
@@ -104,7 +104,7 @@
     lane = lax.broadcasted_iota(jnp.int32, (p, 8 * p), 1)
     unit = lax.broadcasted_iota(jnp.int32, (p, 8 * p), 0)
     tile = jnp.where(lane % p == unit, 1.0, 0.0).astype(BF16)
-    repeated = dot(wl_ref[...], tile)
+    repeated = dot(turned(wl_ref), tile)
     group = lax.broadcasted_iota(jnp.int32, repeated.shape, 1) // p
     total = None
     for i in range(8):
@@ -236,9 +236,8 @@
     await_bytes(every.at[:, :, 0], send_sem.at[4])
 
 
-def outer_and_gates(mine, mine_wide, wide, out_w, pair, weights, stack, mid_all, normed_all, acc, sides):
-    rows, cols, width = pair.shape
-    factor = mine.shape[2] // rows
+def outer_sums(mine, mine_wide, wide, stack):
+    rows, factor, cols = stack.shape[0], mine.shape[2] // stack.shape[0], stack.shape[2]
     seqs = NZ * NS
     for h in range(2):
         mine_wide[h] = mine[:, :, lanes(h)].astype(F32).reshape(seqs, 128)
@@ -252,7 +251,7 @@
         axis=0,
     ).astype(BF16)
 
-    @pl.loop(0, factor)
+    @pl.loop(0, factor, unroll=4)
     def _(q):
         part = jnp.concatenate(
             [wide[h, pl.ds(q, seqs, stride=factor), :] for h in range(2)], axis=1
@@ -261,64 +260,74 @@
         at = pl.ds(pl.multiple_of(q * factor, factor), factor)
         stack[:, at, :] = outer.astype(BF16).reshape(rows, factor, cols)
 
-    wl, wlg, wr, wrg = (turned(ref) for ref in weights)
-    hidden = wl.shape[0]
-
-    @pl.loop(0, rows)
+
+def gated(gate, value, normed, acc, i):
+    rows = acc.shape[1] // value.shape[0]
+    side = jax.nn.sigmoid(dot(gate, normed)) * dot(value, normed)
+    for h in range(2):
+        acc[h, pl.ds(i, value.shape[0], stride=rows), :] = side[:, lanes(h)]
+
+
+def put_side(acc, side):
+    for h in range(2):
+        side[:, :, :, lanes(h)] = split_rows(acc[h]).reshape(side.shape[:3] + (128,))
+
+
+def right_gates(out_w, pair, gate_ref, value_ref, stack, mid_all, normed_all, acc, side):
+    gate, value = turned(gate_ref), turned(value_ref)
+
+    @pl.loop(0, pair.shape[0], unroll=2)
     def _(i):
         mid = (dot(out_w[...], stack[i]) + pair[i].astype(F32).T).astype(BF16)
         mid_all[i] = mid
         normed = layer_norm(mid, 0).astype(BF16)
         normed_all[i] = normed
-        for k, (gate, value) in enumerate(((wlg, wl), (wrg, wr))):
-            side = jax.nn.sigmoid(dot(gate, normed)) * dot(value, normed)
-            for h in range(2):
-                acc[k, h, pl.ds(i, hidden, stride=rows), :] = side[:, lanes(h)]
-
-    for k in range(2):
-        for h in range(2):
-            sides[k][:, :, :, lanes(h)] = split_rows(acc[k, h]).reshape(NZ, NS, rows, 128)
-
-
-def first_legs(me, a_in, b_in, a_mid, b_mid, send_sem, a_sem, b_sem):
-    z, s = me.z, me.s
-    keep(a_in.at[:, s], a_mid.at[s], a_sem)
-    keep(b_in.at[z], b_mid.at[z], b_sem)
+        gated(gate, value, normed, acc, i)
+
+    put_side(acc, side)
+
+
+def left_gates(gate_ref, value_ref, normed_all, acc, side):
+    gate, value = turned(gate_ref), turned(value_ref)
+
+    @pl.loop(0, normed_all.shape[0], unroll=2)
+    def _(i):
+        gated(gate, value, normed_all[i], acc, i)
+
+    put_side(acc, side)
+
+
+def along_y(me, src, dst, send_sem, sem):
+    keep(src(me.s), dst, sem)
     for t in range(1, NS):
-        st = (s + t) % NS
-        send(a_in.at[:, st], a_mid.at[s], send_sem.at[0], a_sem, me.at(s=st))
-        if t <= len(HOPS):
-            zt = (z + HOPS[t - 1]) % NZ
-            send(b_in.at[zt], b_mid.at[z], send_sem.at[1], b_sem, me.at(z=zt))
-
-
-def sent_legs(a_mid, b_mid, send_sem):
-    await_bytes(a_mid.at[pl.ds(0, NS - 1)], send_sem.at[0])
-    await_bytes(b_mid.at[pl.ds(0, NZ - 1)], send_sem.at[1])
-    await_bytes(a_mid.at[:, pl.ds(0, NZ - 1)], send_sem.at[2])
-    await_bytes(b_mid.at[:, pl.ds(0, NS - 1)], send_sem.at[3])
+        st = (me.s + t) % NS
+        send(src(st), dst, send_sem, sem, me.at(s=st))
+
+
+def along_z(me, src, dst, send_sem, sem):
+    keep(src(me.z), dst, sem)
+    for t in HOPS:
+        zt = (me.z + t) % NZ
+        send(src(zt), dst, send_sem, sem, me.at(z=zt))
+
+
+ORDER = (0,) + HOPS
+FROM_LEFT = (0, 5, 6, 7)
 
 
 def spread(me, a_in, b_in, a_out, b_out, a_mid, b_mid, b_all, sems):
     send_sem, first_sem, a_sem, b_sem, right_sem, left_sem, far_sem, side_sem = sems
     z, s, x = me.z, me.s, me.x
-    first_legs(me, a_in, b_in, a_mid, b_mid, send_sem, first_sem.at[0], first_sem.at[1])
+    await_bytes(b_mid, first_sem.at[1])
+    along_y(me, lambda st: b_mid.at[:, st], b_all.at[:, s], send_sem.at[3], b_sem.at[s])
     await_bytes(a_mid, first_sem.at[0])
-    keep(a_mid.at[:, z], a_out.at[x, z], a_sem.at[z])
-    for t in HOPS:
-        zt = (z + t) % NZ
-        send(a_mid.at[:, zt], a_out.at[x, z], send_sem.at[2], a_sem.at[z], me.at(z=zt))
-    await_bytes(b_mid, first_sem.at[1])
-    keep(b_mid.at[:, s], b_all.at[:, s], b_sem)
-    for t in range(1, NS):
-        st = (s + t) % NS
-        send(b_mid.at[:, st], b_all.at[:, s], send_sem.at[3], b_sem, me.at(s=st))
+    along_z(me, lambda zt: a_mid.at[:, zt], a_out.at[x, z], send_sem.at[2], a_sem.at[z])
 
     after, before = (x + 1) % NX, (x + 3) % NX
 
     def pass_on(t):
         zt = (z + t) % NZ
-        if t in (0, 5, 6, 7):
+        if t in FROM_LEFT:
             part = a_out.at[before, zt]
             await_bytes(part, left_sem.at[zt])
             send(part, part, send_sem.at[5], far_sem.at[zt], me.at(x=after))
@@ -327,36 +336,42 @@
             await_bytes(part, right_sem.at[zt])
             send(part, part, send_sem.at[5], far_sem.at[zt], me.at(x=before))
 
-    order = (0,) + HOPS
-    for k, t in enumerate(order):
+    for k, t in enumerate(ORDER):
+        for u in (2 * k, 2 * k + 1):
+            su = (s + NS - u) % NS
+            await_bytes(b_all.at[:, su], b_sem.at[su])
+            for d in (1, 3, 2):
+                xt = (x + d) % NX
+                send(
+                    b_all.at[pl.ds(2 * xt, 2), su],
+                    b_out.at[x, :, su],
+                    send_sem.at[6],
+                    side_sem,
+                    me.at(x=xt),
+                )
         zt = (z + t) % NZ
         part = a_out.at[x, zt]
         await_bytes(part, a_sem.at[zt])
         send(part, part, send_sem.at[4], left_sem.at[zt], me.at(x=after))
         send(part, part, send_sem.at[4], right_sem.at[zt], me.at(x=before))
         if k >= 2:
-            pass_on(order[k - 2])
-    await_bytes(b_all, b_sem)
+            pass_on(ORDER[k - 2])
     keep(b_all.at[pl.ds(2 * x, 2)], b_out.at[x], side_sem)
-    for t in range(1, NX):
-        xt = (x + t) % NX
-        send(b_all.at[pl.ds(2 * xt, 2)], b_out.at[x], send_sem.at[6], side_sem, me.at(x=xt))
-    for t in order[-2:]:
-        pass_on(t)
-    await_bytes(b_out, side_sem)
-
-
-def multiply(me, a_out, b_out, product, cols_all, sems):
-    right_sem, left_sem, far_sem = sems
-    order = (0,) + HOPS
-    rows = b_out.shape[1] * b_out.shape[2] * b_out.shape[3]
-    for k in range(NX):
-        cols_all[k] = flat_rows(b_out.at[k])
-    for t in order:
-        zt = (me.z + t) % NZ
-        part = a_out.at[me.x, zt]
+    return pass_on
+
+
+def multiply_and_return(
+    me, pass_on, a_out, b_out, cols_all, product, y_mid, z_mid, final, arrive_sems, sems
+):
+    right_sem, left_sem, far_sem, side_sem = arrive_sems
+    send_sem, y_sem, z_sem, final_sem = sems
+    z, s, x = me.z, me.s, me.x
+
+    def first(t):
+        zt = (z + t) % NZ
+        part = a_out.at[x, zt]
         await_bytes(part, far_sem.at[zt])
-        await_bytes(part, (right_sem if t in (0, 5, 6, 7) else left_sem).at[zt])
+        await_bytes(part, (right_sem if t in FROM_LEFT else left_sem).at[zt])
         total = None
         for k in range(NX):
             term = lax.dot_general(
@@ -366,32 +381,47 @@
                 preferred_element_type=F32,
             )
             total = term if total is None else total + term
-        for h in range(2):
-            product[h][zt] = split_rows(total[:, lanes(h)])
-
-
-def bring_back(me, a_in, b_in, a_out, b_out, a_mid, b_mid, sems):
-    send_sem, first_sem, last_sem = sems
-    z, s = me.z, me.s
-    first_legs(me, a_in, b_in, a_mid, b_mid, send_sem, first_sem.at[0], first_sem.at[1])
-    await_bytes(a_mid, first_sem.at[0])
-    keep(a_mid.at[:, z], a_out.at[z], last_sem.at[0])
-    for t in HOPS:
-        zt = (z + t) % NZ
-        send(a_mid.at[:, zt], a_out.at[z], send_sem.at[2], last_sem.at[0], me.at(z=zt))
-    await_bytes(b_mid, first_sem.at[1])
-    keep(b_mid.at[:, s], b_out.at[:, s], last_sem.at[1])
-    for t in range(1, NS):
-        st = (s + t) % NS
-        send(b_mid.at[:, st], b_out.at[:, s], send_sem.at[3], last_sem.at[1], me.at(s=st))
-    await_bytes(a_out, last_sem.at[0])
-    await_bytes(b_out, last_sem.at[1])
+        product[zt] = split_rows(total)
+        if t == 0:
+            along_y(me, lambda st: product.at[zt, st], final.at[z, s], send_sem.at[0], final_sem)
+        elif t % 2 == 0:
+            along_y(
+                me, lambda st: product.at[zt, st], y_mid.at[zt, s], send_sem.at[0], y_sem.at[zt]
+            )
+        else:
+            send(product.at[zt], z_mid.at[z], send_sem.at[2], z_sem.at[z], me.at(z=zt))
+
+    def second(t):
+        if t == 0:
+            return
+        if t % 2 == 0:
+            zt = (z + t) % NZ
+            await_bytes(y_mid.at[zt], y_sem.at[zt])
+            send(y_mid.at[zt], final.at[z], send_sem.at[1], final_sem, me.at(z=zt))
+        else:
+            zf = (z + NZ - t) % NZ
+            await_bytes(z_mid.at[zf], z_sem.at[zf])
+            along_y(me, lambda st: z_mid.at[zf, st], final.at[zf, s], send_sem.at[3], final_sem)
+
+    pass_on(ORDER[6])
+    await_bytes(b_out, side_sem)
+    for k in range(NX):
+        cols_all[k] = flat_rows(b_out.at[k])
+    for k, t in enumerate(ORDER):
+        first(t)
+        if k == 1:
+            pass_on(ORDER[7])
+        if k >= 2:
+            second(ORDER[k - 2])
+    second(ORDER[6])
+    second(ORDER[7])
+    await_bytes(final, final_sem)
 
 
 def finish(parts, wide, mid_all, normed_all, gate_ref, out_ref, result):
     rows, width, cols = mid_all.shape
-    for h, ref in enumerate(parts):
-        wide[h] = ref[...].astype(F32).reshape(-1, 128)
+    for h in range(2):
+        wide[h] = parts[:, :, :, lanes(h)].astype(F32).reshape(-1, 128)
     hidden = wide.shape[1] // rows
     gate_w, out_w = turned(gate_ref), turned(out_ref)
 
@@ -443,12 +473,10 @@
     a_out,
     b_out,
     cols_all,
-    product_a,
-    product_b,
-    pa_mid,
-    pb_mid,
-    pa_out,
-    pb_out,
+    product,
+    y_mid,
+    z_mid,
+    final,
     load_sem,
     g_send,
     g_first,
@@ -464,8 +492,9 @@
     s_far,
     s_side,
     r_send,
-    r_first,
-    r_last,
+    r_y,
+    r_z,
+    r_final,
 ):
     me = Place()
     count = greet_all(me)
@@ -478,8 +507,8 @@
         await_bytes(opm_out, load_sem.at[1])
         await_bytes(pair, load_sem.at[0])
         opm_wide[...] = opm_out[...].astype(F32)
-        p = opm_left_ref.shape[1]
-        q = opm_right_ref.shape[1]
+        p = opm_left_ref.shape[0]
+        q = opm_right_ref.shape[0]
         for k in range(q):
             rows = opm_wide[pl.ds(k, p, stride=q), :]
             mine_rows = slice(k * p, (k + 1) * p)
@@ -499,20 +528,22 @@
         prepare,
         (g_send, g_first, g_next, g_twin, g_left),
     )
-    outer_and_gates(
-        mine,
-        half_wide,
-        wide,
+    outer_sums(mine, half_wide, wide, stack)
+    right_gates(
         out_w,
         pair,
-        (tri_left_ref, tri_left_gate_ref, tri_right_ref, tri_right_gate_ref),
+        tri_right_gate_ref,
+        tri_right_ref,
         stack,
         mid_all,
         normed_all,
-        acc,
-        (left_side, right_side),
+        acc.at[1],
+        right_side,
     )
-    spread(
+    along_z(me, lambda zt: right_side.at[zt], b_mid.at[me.z], s_send.at[1], s_first.at[1])
+    left_gates(tri_left_gate_ref, tri_left_ref, normed_all, acc.at[0], left_side)
+    along_y(me, lambda st: left_side.at[:, st], a_mid.at[me.s], s_send.at[0], s_first.at[0])
+    pass_on = spread(
         me,
         left_side,
         right_side,
@@ -523,17 +554,31 @@
         b_all,
         (s_send, s_first, s_a, s_b, s_right, s_left, s_far, s_side),
     )
-    multiply(me, a_out, b_out, (product_a, product_b), cols_all, (s_right, s_left, s_far))
-    bring_back(
-        me, product_a, product_b, pa_out, pb_out, pa_mid, pb_mid, (r_send, r_first, r_last)
+    multiply_and_return(
+        me,
+        pass_on,
+        a_out,
+        b_out,
+        cols_all,
+        product,
+        y_mid,
+        z_mid,
+        final,
+        (s_right, s_left, s_far, s_side),
+        (r_send, r_y, r_z, r_final),
     )
-    finish((pa_out, pb_out), acc.at[0], mid_all, normed_all, tri_gate_ref, tri_out_ref, result)
-
-    sent_legs(a_mid, b_mid, s_send)
+    finish(final, acc.at[0], mid_all, normed_all, tri_gate_ref, tri_out_ref, result)
+    await_bytes(a_mid.at[pl.ds(0, NS - 1)], s_send.at[0])
+    await_bytes(b_mid.at[pl.ds(0, NZ - 1)], s_send.at[1])
+    await_bytes(a_mid.at[:, pl.ds(0, NZ - 1)], s_send.at[2])
+    await_bytes(b_mid.at[:, pl.ds(0, NS - 1)], s_send.at[3])
     await_bytes(a_out.at[pl.ds(0, 2)], s_send.at[4])
     await_bytes(a_out.at[0], s_send.at[5])
     await_bytes(b_out.at[pl.ds(0, NX - 1)], s_send.at[6])
-    sent_legs(pa_mid, pb_mid, r_send)
+    await_bytes(final.at[pl.ds(0, 4), pl.ds(0, NS - 1)], r_send.at[0])
+    await_bytes(final.at[pl.ds(0, 3)], r_send.at[1])
+    await_bytes(final.at[pl.ds(0, 4)], r_send.at[2])
+    await_bytes(final.at[pl.ds(0, 4), pl.ds(0, NS - 1)], r_send.at[3])
 
 
 def on_device(pair, alignment, opm_left, opm_right, opm_out, *weights):
@@ -575,12 +620,10 @@
         vb(NX, NZ, NS, rows, cols),
         vb(NX, NZ // NX, NS, rows, cols),
         vb(NX, cols, cols),
-        vb(NZ, NS, rows, 128),
-        vb(NZ, NS, rows, 128),
-        vb(NS, NZ, rows, 128),
-        vb(NZ, NS, rows, 128),
-        vb(NZ, NS, rows, 128),
-        vb(NZ, NS, rows, 128),
+        vb(NZ, NS, rows, cols),
+        vb(NZ, NS, rows, cols),
+        vb(NZ, NS, rows, cols),
+        vb(NZ, NS, rows, cols),
         DMA((2,)),
         DMA((5,)),
         DMA,
@@ -590,14 +633,15 @@
         DMA((7,)),
         DMA((2,)),
         DMA((NZ,)),
-        DMA,
+        DMA((NS,)),
         DMA((NZ,)),
         DMA((NZ,)),
         DMA((NZ,)),
         DMA,
         DMA((4,)),
-        DMA((2,)),
-        DMA((2,)),
+        DMA((NZ,)),
+        DMA((NZ,)),
+        DMA,
     ]
     return pl.pallas_call(
         kernel,
@@ -609,7 +653,7 @@
             collective_id=0, has_side_effects=True, vmem_limit_bytes=56 << 20
         ),
         name="evoformer_pair",
-    )(pair, opm_out, alignment, opm_left, opm_right, *weights)
+    )(pair, opm_out, alignment, opm_left.T, opm_right.T, *weights)
 
 
 def solution(mesh):

time: 127 us -> 122 us (0.961)
  local copies, waits for them, and re-layouts: 4.08 us -> 1.87 us
  Pallas kernels: 122 us -> 120 us
    unnamed x5 -> x1, local copies, waits for them, and re-layouts: 4.08 us -> 1.87 us
    pallas_call x1, Pallas kernels: 122 us -> 120 us  [on_device(): pl.pallas_call(kernel, out_shape=jax.ShapeDtypeStruct((rows, cols, width)...]
where the time goes in v3:
time: 122 us
  Pallas kernels  120 us (98%)
  local copies, waits for them, and re-layouts  1.87 us (2%)
    pallas_call x1, Pallas kernels, on_device(): pl.pallas_call(kernel, out_shape=jax.ShapeDtypeStruct((rows, cols, width)...  120 us

profile of v3, /device:TPU:1, one launch (start us, length us, event | category | flops | bytes accessed | tf_op | source)
XLA Modules:
  0.0 122.0 jit_solution(15043336996334320866)
XLA Ops:
  0.0 120.1 %evoformer_pair.1 = bf16[8,256,128]{2,1,0:T(8,128)(2,1)} custom-call(bf16[8,256,128]{2,1,0:T(8,128)(2,1)} %pair_hbm.1, bf16[1024,128]{1,0:T(8,128)(2,1)} %opm_out_hbm.1, bf16[1,256,256]{2,1,0:T(8,128)(2,1)} %align_ref.1, bf16[32,256]{1,0:T(8,128)(2,1)} %bitcast.2, bf16[32,256]{1,0:T(8,128)(2,1)} %bitcast.3, bf16[128,128]{1,0:T(8,128)(2,1)} %tri_left_ref.1, ...), custom_call_target="tpu_custom_call" | custom-call | tf_op jit(solution)/shard_map/evoformer_pair/pallas_call | solution.py:646
  120.1 1.9 %copy.13 = bf16[8,256,128]{2,1,0:T(8,128)(2,1)} copy(bf16[8,256,128]{2,1,0:T(8,128)(2,1)} %evoformer_pair.1) | data formatting | bytes 1048576

commit v4 on v3

v4 whole, which is shorter than its diff:
```python
import jax
import jax.numpy as jnp
from jax import lax
from jax.experimental import pallas as pl
from jax.experimental.pallas import tpu as pltpu
from jax.sharding import PartitionSpec as P

EPS = 1e-05
MESH = pl.DeviceIdType.MESH
F32 = jnp.float32
BF16 = jnp.bfloat16
VMEM = pl.BlockSpec(memory_space=pltpu.VMEM)
ANY = pl.BlockSpec(memory_space=pl.ANY)
DMA = pltpu.SemaphoreType.DMA

NX = 4
NZ = 8
NQ = 8
NS = 2 * NQ
NY = NS // 2
HOPS = (1, 7, 2, 6, 3, 5, 4)


class Place:
    def __init__(self):
        row = lax.axis_index("row")
        self.x = lax.axis_index("col")
        seq = lax.axis_index("seq")
        self.z = row // 2
        self.s = (row % 2) * NQ + seq
        self.yy = self.s // 2
        self.core = self.s % 2

    def at(self, z=None, s=None, x=None):
        z = self.z if z is None else z
        s = self.s if s is None else s
        x = self.x if x is None else x
        return (z * 2 + s // NQ, x, s % NQ)


def send(src, dst, send_sem, recv_sem, device):
    pltpu.make_async_remote_copy(
        src_ref=src,
        dst_ref=dst,
        send_sem=send_sem,
        recv_sem=recv_sem,
        device_id=device,
        device_id_type=MESH,
    ).start()


def keep(src, dst, sem):
    pltpu.make_async_copy(src, dst, sem).start()


def await_bytes(ref, sem):
    pltpu.make_async_copy(ref, ref, sem).wait()


def greet(device):
    pl.semaphore_signal(
        pltpu.get_barrier_semaphore(), inc=1, device_id=device, device_id_type=MESH
    )


def layer_norm(values, axis):
    values = values.astype(F32)
    center = values - jnp.mean(values, axis=axis, keepdims=True)
    spread = jnp.mean(center * center, axis=axis, keepdims=True)
    return center * lax.rsqrt(spread + EPS)


def turned(ref):
    return ref[...].astype(F32).T.astype(BF16)


def dot(a, b):
    return jnp.dot(a, b, preferred_element_type=F32)


def lanes(h):
    return slice(h * 128, (h + 1) * 128)


def flat_rows(ref):
    values = ref[...].astype(F32)
    return values.reshape(-1, values.shape[-1]).astype(BF16)


def split_rows(values):
    return values.reshape(-1, 8, values.shape[-1]).astype(BF16)


def factors(align_ref, wl_ref, wr_ref, normed, left_own, right_own):
    cols, width = align_ref.shape[1:]
    p = wl_ref.shape[0]
    seq = layer_norm(align_ref[0], 1).astype(BF16)
    right_own[...] = lax.dot_general(
        wr_ref[...], seq, (((1,), (1,)), ((), ())), preferred_element_type=F32
    ).astype(BF16)
    wide = seq.astype(F32)
    for h in range(width // 128):
        normed[h] = wide[:, lanes(h)]
    lane = lax.broadcasted_iota(jnp.int32, (p, 8 * p), 1)
    unit = lax.broadcasted_iota(jnp.int32, (p, 8 * p), 0)
    tile = jnp.where(lane % p == unit, 1.0, 0.0).astype(BF16)
    repeated = dot(turned(wl_ref), tile)
    group = lax.broadcasted_iota(jnp.int32, repeated.shape, 1) // p
    total = None
    for i in range(8):
        rows = jnp.concatenate(
            [normed[h, pl.ds(i, cols // 8, stride=8), :] for h in range(width // 128)], axis=1
        ).astype(BF16)
        term = dot(rows, jnp.where(group == i, repeated, 0.0).astype(BF16))
        total = term if total is None else total + term
    left_own[...] = total.astype(BF16).reshape(left_own.shape)


def greet_all(me):
    for t in range(1, NS):
        greet(me.at(s=(me.s + t) % NS))
    for t in range(1, NZ):
        greet(me.at(z=(me.z + t) % NZ))
    for t in range(1, NX):
        greet(me.at(x=(me.x + t) % NX))
    owner = me.z // 2
    for t in range(NZ):

        @pl.when(jnp.logical_not(jnp.logical_and(owner == me.x, me.z == t)))
        def _():
            greet(me.at(z=t, x=owner))

    return NS - 1 + NZ - 1 + NX - 1 + 8 - jnp.where(owner == me.x, 1, 0)


def gather(me, left_own, right_own, half, half_wide, mine_send, mine, every, wide, sems):
    send_sem, first_sem, next_sem, twin_sem, left_sem = sems
    z, s, x, yy, core = me.z, me.s, me.x, me.yy, me.core
    q = right_own.shape[0]
    here = jnp.where(z // 2 == x, 1, 0)

    own = every.at[z, yy, core]
    keep(right_own, own, first_sem)

    @pl.when(core == 0)
    def _():
        for t in HOPS:
            send(right_own, own, send_sem.at[1], first_sem, me.at(z=(z + t) % NZ))

    @pl.when(core == 1)
    def _():
        for t in HOPS:
            send(right_own, own, send_sem.at[1], first_sem, me.at(s=(s + 2 * t) % NS))

    for h in range(2):
        for xt in range(NX):
            zt = 2 * x + h
            same = jnp.logical_and(x == xt, z == zt)

            @pl.when(same)
            def _():
                keep(left_own.at[h], half.at[z], left_sem.at[0])

            @pl.when(jnp.logical_not(same))
            def _():
                send(left_own.at[h], half.at[z], send_sem.at[0], left_sem.at[0], me.at(z=zt, x=xt))

    await_bytes(every.at[:, 0, 0], first_sem)
    twin = me.at(s=s + 1 - 2 * core)

    def line(c, p, half_line):
        at = pl.ds(4 * half_line, 4)
        return every.at[at, index_of(c, p), 0] if c == 0 else every.at[index_of(c, p), at, 1]

    def index_of(c, p):
        return p % 2 * 4 + p // 2 if c == 0 else p

    def place_of(c):
        return yy % 4 * 2 + yy // 4 if c == 0 else z

    def peer(c, p):
        return me.at(s=2 * index_of(c, p)) if c == 0 else me.at(z=p)

    def widen(c, p, half_line):
        @pl.loop(0, 4)
        def _(j):
            n = (4 * half_line + j) * NS + 2 * index_of(c, p)
            if c == 1:
                n = index_of(c, p) * NS + 2 * (4 * half_line + j) + 1
            at = pl.ds(pl.multiple_of(n * q, q), q)
            block = line(c, p, half_line)[j].astype(F32)
            for h in range(2):
                wide[h, at, :] = block[:, lanes(h)]

    events = [
        (d, way, half_line)
        for d in range(1, 5)
        for half_line in range(2)
        for way in range(2)
        if d <= 3 + (way == half_line)
    ]

    def moved(c, d, way):
        return (place_of(c) + (NZ - d if way == 0 else d)) % NZ

    for c in range(2):

        @pl.when(core == c)
        def _(c=c):
            here_p = place_of(c)
            ends = ((here_p + 1) % NZ, (here_p + NZ - 1) % NZ)
            for half_line in range(2):
                part = line(c, here_p, half_line)
                for end in ends:
                    send(
                        part,
                        part,
                        send_sem.at[3],
                        next_sem.at[index_of(c, here_p), half_line],
                        peer(c, end),
                    )
                send(
                    part,
                    part,
                    send_sem.at[4],
                    twin_sem.at[index_of(c, here_p), half_line],
                    twin,
                )

    await_bytes(half, left_sem.at[0])
    for h in range(2):
        half_wide[h] = half[:, :, lanes(h)].astype(F32).reshape(NZ * NS, 128)
    for b in range(NS):
        mine_send[b] = jnp.concatenate(
            [half_wide[h, pl.ds(b, NZ, stride=NS), :] for h in range(2)], axis=1
        ).astype(BF16)
    keep(mine_send.at[s], mine.at[s], left_sem.at[1])
    for t in range(1, NS):
        st = (s + t) % NS
        send(mine_send.at[st], mine.at[s], send_sem.at[2], left_sem.at[1], me.at(s=st))

    for c in range(2):

        @pl.when(core == c)
        def _(c=c):
            here_p = place_of(c)
            ends = ((here_p + 1) % NZ, (here_p + NZ - 1) % NZ)
            steps = [(here_p, 0, 0, 0), (here_p, 0, 0, 1)] + [
                (moved(c, d, way), d, way, half_line) for d, way, half_line in events
            ]
            far_p = place_of(1 - c)
            far_steps = [(far_p, 0), (far_p, 1)] + [
                (moved(1 - c, d, way), half_line) for d, way, half_line in events
            ]

            def from_twin(k):
                p, half_line = far_steps[k]
                part = line(1 - c, p, half_line)
                await_bytes(part, twin_sem.at[index_of(1 - c, p), half_line])
                widen(1 - c, p, half_line)

            for k, (p, d, way, half_line) in enumerate(steps):
                part = line(c, p, half_line)
                if d:
                    sem = next_sem.at[index_of(c, p), half_line]
                    await_bytes(part, sem)
                    if d < 3 + (way == half_line):
                        send(part, part, send_sem.at[3], sem, peer(c, ends[way]))
                    send(
                        part,
                        part,
                        send_sem.at[4],
                        twin_sem.at[index_of(c, p), half_line],
                        twin,
                    )
                widen(c, p, half_line)
                if k >= 4:
                    from_twin(k - 4)
            for k in range(len(steps) - 4, len(steps)):
                from_twin(k)

    await_bytes(mine, left_sem.at[1])

    @pl.when(here == 1)
    def _():
        await_bytes(half.at[pl.ds(0, 7)], send_sem.at[0])

    @pl.when(here == 0)
    def _():
        await_bytes(half, send_sem.at[0])

    await_bytes(every.at[pl.ds(0, 7), 0, 0], send_sem.at[1])
    await_bytes(mine.at[pl.ds(0, NS - 1)], send_sem.at[2])
    await_bytes(every.at[pl.ds(0, 7), :, 0], send_sem.at[3])
    await_bytes(every.at[:, :, 0], send_sem.at[4])


def outer_sums(mine, mine_wide, wide, stack):
    rows, factor, cols = stack.shape[0], mine.shape[2] // stack.shape[0], stack.shape[2]
    seqs = NZ * NS
    for h in range(2):
        mine_wide[h] = mine[:, :, lanes(h)].astype(F32).reshape(seqs, 128)
    left = jnp.concatenate(
        [
            jnp.concatenate(
                [mine_wide[h, pl.ds(z, NS, stride=NZ), :] for z in range(NZ)], axis=0
            ).T
            for h in range(2)
        ],
        axis=0,
    ).astype(BF16)

    @pl.loop(0, factor, unroll=4)
    def _(q):
        part = jnp.concatenate(
            [wide[h, pl.ds(q, seqs, stride=factor), :] for h in range(2)], axis=1
        ).astype(BF16)
        outer = dot(left, part) * (1.0 / seqs)
        at = pl.ds(pl.multiple_of(q * factor, factor), factor)
        stack[:, at, :] = outer.astype(BF16).reshape(rows, factor, cols)


def gated(gate, value, normed, acc, i):
    rows = acc.shape[1] // value.shape[0]
    side = jax.nn.sigmoid(dot(gate, normed)) * dot(value, normed)
    for h in range(2):
        acc[h, pl.ds(i, value.shape[0], stride=rows), :] = side[:, lanes(h)]


def put_side(acc, side):
    for h in range(2):
        side[h] = split_rows(acc[h]).reshape(side.shape[1:])


def left_gates(out_w, pair, gate_ref, value_ref, stack, mid_all, normed_all, acc, side):
    gate, value = turned(gate_ref), turned(value_ref)

    @pl.loop(0, pair.shape[0], unroll=2)
    def _(i):
        mid = (dot(out_w[...], stack[i]) + pair[i].astype(F32).T).astype(BF16)
        mid_all[i] = mid
        normed = layer_norm(mid, 0).astype(BF16)
        normed_all[i] = normed
        gated(gate, value, normed, acc, i)

    put_side(acc, side)


def right_gates(gate_ref, value_ref, normed_all, acc, side):
    gate, value = turned(gate_ref), turned(value_ref)

    @pl.loop(0, normed_all.shape[0], unroll=2)
    def _(i):
        gated(gate, value, normed_all[i], acc, i)

    put_side(acc, side)


def along_y(me, src, dst, send_sem, sem, offsets=range(NS)):
    for t in offsets:
        if t == 0:
            keep(src(me.s), dst, sem)
        else:
            st = (me.s + t) % NS
            send(src(st), dst, send_sem, sem, me.at(s=st))


def along_z(me, src, dst, send_sem, sem, offsets=(0,) + HOPS):
    for t in offsets:
        if t == 0:
            keep(src(me.z), dst, sem)
        else:
            zt = (me.z + t) % NZ
            send(src(zt), dst, send_sem, sem, me.at(z=zt))


ORDER = (0,) + HOPS
UNITS = NZ + NS
LAG = 8


def left_legs(me, side, y_mid, z_mid, out, sems):
    send_sem, first_sem, z_sem, s_sem = sems
    await_bytes(y_mid, first_sem.at[0])
    along_z(me, lambda zt: y_mid.at[:, zt], out.at[0, me.z], send_sem.at[2], z_sem.at[me.z])
    await_bytes(z_mid, first_sem.at[1])
    along_y(me, lambda st: z_mid.at[:, st], out.at[1, :, me.s], send_sem.at[3], s_sem.at[me.s])


def first_legs(me, side, y_mid, z_mid, send_sem, first_sem, parts=(0, 1)):
    for part in parts:
        along_y(
            me,
            lambda st: side.at[0, :, st],
            y_mid.at[me.s],
            send_sem.at[0],
            first_sem.at[0],
            range(part, NS, 2),
        )
        along_z(
            me,
            lambda zt: side.at[1, zt],
            z_mid.at[me.z],
            send_sem.at[1],
            first_sem.at[1],
            ORDER[4 * part : 4 * part + 4],
        )


def legs_left(y_mid, z_mid, send_sem):
    await_bytes(y_mid.at[pl.ds(0, NS - 1)], send_sem.at[0])
    await_bytes(z_mid.at[pl.ds(0, NZ - 1)], send_sem.at[1])
    await_bytes(y_mid.at[:, pl.ds(0, NZ - 1)], send_sem.at[2])
    await_bytes(z_mid.at[:, pl.ds(0, NS - 1)], send_sem.at[3])


def spread(me, left_side, right_side, right_gates, a_out, rows_all, b_all, b_out, mids, l_sems, r_sems, x_sems):
    z, s, x = me.z, me.s, me.x
    ly_mid, lz_mid, ry_mid, rz_mid = mids
    x_send, near_sem, far_sem, side_sem = x_sems
    first_legs(me, left_side, ly_mid, lz_mid, l_sems[0], l_sems[1])
    right_gates()
    first_legs(me, right_side, ry_mid, rz_mid, r_sems[0], r_sems[1], (0,))
    left_legs(me, left_side, ly_mid, lz_mid, a_out.at[:, x], l_sems)
    first_legs(me, right_side, ry_mid, rz_mid, r_sems[0], r_sems[1], (1,))

    after, before = (x + 1) % NX, (x + 3) % NX

    def unit(k):
        if k < NZ:
            zt = (z + ORDER[k]) % NZ
            return zt, lambda xt: a_out.at[0, xt, zt], l_sems[2].at[zt]
        st = (s + 2 * NS - k + NZ) % NS
        return NZ + st, lambda xt: a_out.at[1, xt, :, st], l_sems[3].at[st]

    def pass_on(k):
        n, place, _ = unit(k)
        way = k % 2
        part = place(after if way else before)
        await_bytes(part, near_sem.at[way, n])
        send(part, part, x_send.at[1], far_sem.at[n], me.at(x=before if way else after))

    for k in range(UNITS):
        n, place, sem = unit(k)
        part = place(x)
        await_bytes(part, sem)
        send(part, part, x_send.at[0], near_sem.at[0, n], me.at(x=after))
        send(part, part, x_send.at[0], near_sem.at[1, n], me.at(x=before))
        if k >= LAG:
            pass_on(k - LAG)
        if k == UNITS - 8:
            left_legs(me, right_side, ry_mid, rz_mid, b_all, r_sems)
    for k in range(UNITS - LAG, UNITS):
        pass_on(k)

    for k in range(NZ):
        zt = (z + ORDER[k]) % NZ
        xt = zt // 2
        part, there = b_all.at[0, zt], b_out.at[0, x, zt % 2]
        await_bytes(part, r_sems[2].at[zt])

        @pl.when(xt == x)
        def _():
            keep(part, there, side_sem)

        @pl.when(xt != x)
        def _():
            send(part, there, x_send.at[2], side_sem, me.at(x=xt))

        for u in (2 * k, 2 * k + 1):
            su = (s + NS - u) % NS
            await_bytes(b_all.at[1, :, su], r_sems[3].at[su])
            for d in (1, 3, 2):
                xt = (x + d) % NX
                send(
                    b_all.at[1, pl.ds(2 * xt, 2), su],
                    b_out.at[1, x, :, su],
                    x_send.at[2],
                    side_sem,
                    me.at(x=xt),
                )
    keep(b_all.at[1, pl.ds(2 * x, 2)], b_out.at[1, x], side_sem)

    for k in range(UNITS):
        n, place, _ = unit(k)
        part = place(x)
        await_bytes(part, far_sem.at[n])
        await_bytes(part, near_sem.at[1 - k % 2, n])

    @pl.loop(0, NX * NZ, unroll=2)
    def _(k):
        xt, zt = k // NZ, k % NZ
        for h in range(2):
            rows_all[xt, zt, :, lanes(h)] = flat_rows(a_out.at[h, xt, zt])

    await_bytes(b_out, side_sem)


def multiply_and_return(me, rows_all, b_out, cols_all, product, y_mid, z_mid, final, sems):
    send_sem, first_sem, final_sem = sems
    z, s = me.z, me.s
    for k in range(NX):
        for h in range(2):
            cols_all[k, :, lanes(h)] = flat_rows(b_out.at[h, k])
    for t in ORDER:
        zt = (z + t) % NZ
        total = None
        for k in range(NX):
            term = lax.dot_general(
                rows_all[k, zt], cols_all[k], (((1,), (1,)), ((), ())), preferred_element_type=F32
            )
            total = term if total is None else total + term
        for h in range(2):
            product[h, zt] = split_rows(total[:, lanes(h)])
        if t == 0:
            keep(product.at[1, z], z_mid.at[z], first_sem.at[1])
        else:
            send(product.at[1, zt], z_mid.at[z], send_sem.at[1], first_sem.at[1], me.at(z=zt))
    along_y(me, lambda st: product.at[0, :, st], y_mid.at[s], send_sem.at[0], first_sem.at[0])
    await_bytes(z_mid, first_sem.at[1])
    along_y(me, lambda st: z_mid.at[:, st], final.at[1, :, s], send_sem.at[3], final_sem)
    await_bytes(y_mid, first_sem.at[0])
    along_z(me, lambda zt: y_mid.at[:, zt], final.at[0, z], send_sem.at[2], final_sem)
    await_bytes(final, final_sem)


def finish(parts, wide, mid_all, normed_all, gate_ref, out_ref, result):
    rows, width, cols = mid_all.shape
    for h in range(2):
        wide[h] = parts[h].astype(F32).reshape(-1, 128)
    hidden = wide.shape[1] // rows
    gate_w, out_w = turned(gate_ref), turned(out_ref)

    @pl.loop(0, rows)
    def _(i):
        product = jnp.concatenate(
            [wide[h, pl.ds(i, hidden, stride=rows), :] for h in range(2)], axis=1
        )
        normed = layer_norm(product, 0).astype(BF16)
        gate = jax.nn.sigmoid(dot(gate_w, normed_all[i]))
        result[i] = (mid_all[i].astype(F32) + gate * dot(out_w, normed)).T.astype(BF16)


def kernel(
    pair_hbm,
    opm_out_hbm,
    align_ref,
    opm_left_ref,
    opm_right_ref,
    tri_left_ref,
    tri_left_gate_ref,
    tri_right_ref,
    tri_right_gate_ref,
    tri_gate_ref,
    tri_out_ref,
    result,
    pair,
    opm_out,
    opm_wide,
    out_w,
    normed_seq,
    left_own,
    right_own,
    half,
    half_wide,
    mine_send,
    mine,
    every,
    wide,
    stack,
    mid_all,
    normed_all,
    acc,
    left_side,
    right_side,
    ly_mid,
    lz_mid,
    ry_mid,
    rz_mid,
    py_mid,
    pz_mid,
    b_all,
    a_out,
    rows_all,
    b_out,
    cols_all,
    product,
    final,
    load_sem,
    g_send,
    g_first,
    g_next,
    g_twin,
    g_left,
    l_send,
    l_first,
    l_z,
    l_s,
    r_send,
    r_first,
    r_z,
    r_s,
    x_send,
    x_near,
    x_far,
    x_side,
    p_send,
    p_first,
    p_final,
):
    me = Place()
    count = greet_all(me)
    keep(pair_hbm, pair, load_sem.at[0])
    keep(opm_out_hbm, opm_out, load_sem.at[1])
    factors(align_ref, opm_left_ref, opm_right_ref, normed_seq, left_own, right_own)
    await_bytes(opm_out, load_sem.at[1])
    await_bytes(pair, load_sem.at[0])
    opm_wide[...] = opm_out[...].astype(F32)
    p = opm_left_ref.shape[0]
    q = opm_right_ref.shape[0]
    for k in range(q):
        rows = opm_wide[pl.ds(k, p, stride=q), :]
        mine_rows = slice(k * p, (k + 1) * p)
        stack[0, mine_rows, 0:128] = rows.astype(BF16)
    out_w[...] = stack[0, :, 0:128].astype(F32).T.astype(BF16)
    pl.semaphore_wait(pltpu.get_barrier_semaphore(), count)

    gather(
        me,
        left_own,
        right_own,
        half,
        half_wide,
        mine_send,
        mine,
        every,
        wide,
        (g_send, g_first, g_next, g_twin, g_left),
    )
    outer_sums(mine, half_wide, wide, stack)
    left_gates(
        out_w,
        pair,
        tri_left_gate_ref,
        tri_left_ref,
        stack,
        mid_all,
        normed_all,
        acc.at[0],
        left_side,
    )
    spread(
        me,
        left_side,
        right_side,
        lambda: right_gates(
            tri_right_gate_ref, tri_right_ref, normed_all, acc.at[1], right_side
        ),
        a_out,
        rows_all,
        b_all,
        b_out,
        (ly_mid, lz_mid, ry_mid, rz_mid),
        (l_send, l_first, l_z, l_s),
        (r_send, r_first, r_z, r_s),
        (x_send, x_near, x_far, x_side),
    )
    multiply_and_return(
        me, rows_all, b_out, cols_all, product, py_mid, pz_mid, final, (p_send, p_first, p_final)
    )
    finish(final, acc.at[0], mid_all, normed_all, tri_gate_ref, tri_out_ref, result)
    legs_left(ly_mid, lz_mid, l_send)
    legs_left(ry_mid, rz_mid, r_send)
    await_bytes(a_out.at[:, pl.ds(0, 2)], x_send.at[0])
    await_bytes(a_out.at[:, 0], x_send.at[1])
    await_bytes(b_out.at[:, pl.ds(0, NX - 1)], x_send.at[2])
    legs_left(py_mid, pz_mid, p_send)


def on_device(pair, alignment, opm_left, opm_right, opm_out, *weights):
    rows, cols, width = pair.shape
    model = alignment.shape[2]
    factor = opm_left.shape[1]
    hidden = weights[0].shape[1]
    seqs = NZ * NS

    def vb(*shape):
        return pltpu.VMEM(shape, BF16)

    def vf(*shape):
        return pltpu.VMEM(shape, F32)

    scratch = [
        vb(rows, cols, width),
        vb(factor * factor, width),
        vf(factor * factor, width),
        vb(width, factor * factor),
        vf(model // 128, cols, 128),
        vb(2, NS, rows * factor),
        vb(factor, cols),
        vb(NZ, NS, rows * factor),
        vf(2, seqs, 128),
        vb(NS, NZ, rows * factor),
        vb(NS, NZ, rows * factor),
        vb(NZ, NY, 2, factor, cols),
        vf(2, seqs * factor, 128),
        vb(rows, factor * factor, cols),
        vb(rows, width, cols),
        vb(rows, width, cols),
        vf(2, 2, hidden * rows, 128),
        vb(2, NZ, NS, rows, 128),
        vb(2, NZ, NS, rows, 128),
        vb(NS, NZ, rows, 128),
        vb(NZ, NS, rows, 128),
        vb(NS, NZ, rows, 128),
        vb(NZ, NS, rows, 128),
        vb(NS, NZ, rows, 128),
        vb(NZ, NS, rows, 128),
        vb(2, NZ, NS, rows, 128),
        vb(2, NX, NZ, NS, rows, 128),
        vb(NX, NZ, NS * rows, cols),
        vb(2, NX, NZ // NX, NS, rows, 128),
        vb(NX, cols, cols),
        vb(2, NZ, NS, rows, 128),
        vb(2, NZ, NS, rows, 128),
        DMA((2,)),
        DMA((5,)),
        DMA,
        DMA((8, 2)),
        DMA((8, 2)),
        DMA((2,)),
        DMA((4,)),
        DMA((2,)),
        DMA((NZ,)),
        DMA((NS,)),
        DMA((4,)),
        DMA((2,)),
        DMA((NZ,)),
        DMA((NS,)),
        DMA((3,)),
        DMA((2, UNITS)),
        DMA((UNITS,)),
        DMA,
        DMA((4,)),
        DMA((2,)),
        DMA,
    ]
    return pl.pallas_call(
        kernel,
        out_shape=jax.ShapeDtypeStruct((rows, cols, width), BF16),
        in_specs=[ANY, ANY] + [VMEM] * 9,
        out_specs=VMEM,
        scratch_shapes=scratch,
        compiler_params=pltpu.CompilerParams(
            collective_id=0, has_side_effects=True, vmem_limit_bytes=56 << 20
        ),
        name="evoformer_pair",
    )(pair, opm_out, alignment, opm_left.T, opm_right.T, *weights)


def solution(mesh):
    split = P(("row", "seq"), "col", None)
    return jax.shard_map(
        on_device,
        mesh=mesh,
        in_specs=(split, split) + (P(),) * 9,
        out_specs=split,
        check_vma=False,
    )
```

time: 122 us -> 114 us (0.934)
  Pallas kernels: 120 us -> 111 us
    pallas_call x1, Pallas kernels: 120 us -> 111 us  [on_device(): pl.pallas_call(kernel, out_shape=jax.ShapeDtypeStruct((rows, cols, width)...]
where the time goes in v4:
time: 114 us; the launch traced here: 113 us
  Pallas kernels  111 us (97%)
  local copies, waits for them, and re-layouts  1.87 us (2%)
    pallas_call x1, Pallas kernels, on_device(): pl.pallas_call(kernel, out_shape=jax.ShapeDtypeStruct((rows, cols, width)...  111 us

profile of v4, /device:TPU:1, one launch (start us, length us, event | category | flops | bytes accessed | tf_op | source)
XLA Modules:
  0.0 113.3 jit_solution(15341996756604435165)
XLA Ops:
  0.0 111.4 %evoformer_pair.1 = bf16[8,256,128]{2,1,0:T(8,128)(2,1)} custom-call(bf16[8,256,128]{2,1,0:T(8,128)(2,1)} %pair_hbm.1, bf16[1024,128]{1,0:T(8,128)(2,1)} %opm_out_hbm.1, bf16[1,256,256]{2,1,0:T(8,128)(2,1)} %align_ref.1, bf16[32,256]{1,0:T(8,128)(2,1)} %bitcast.2, bf16[32,256]{1,0:T(8,128)(2,1)} %bitcast.3, bf16[128,128]{1,0:T(8,128)(2,1)} %tri_left_ref.1, ...), custom_call_target="tpu_custom_call" | custom-call | tf_op jit(solution)/shard_map/evoformer_pair/pallas_call | solution.py:748
  111.4 1.9 %copy.13 = bf16[8,256,128]{2,1,0:T(8,128)(2,1)} copy(bf16[8,256,128]{2,1,0:T(8,128)(2,1)} %evoformer_pair.1) | data formatting | bytes 1048576

commit v5 on v4

--- a/solution.py
+++ b/solution.py
@@ -194,7 +194,7 @@
 
     events = [
         (d, way, half_line)
-        for d in range(1, 5)
+        for d in (2, 1, 3, 4)
         for half_line in range(2)
         for way in range(2)
         if d <= 3 + (way == half_line)
@@ -208,17 +208,18 @@
         @pl.when(core == c)
         def _(c=c):
             here_p = place_of(c)
-            ends = ((here_p + 1) % NZ, (here_p + NZ - 1) % NZ)
-            for half_line in range(2):
+            for step, half_line in ((2, 0), (2, 1), (1, 0), (1, 1)):
                 part = line(c, here_p, half_line)
-                for end in ends:
+                for end in (step, NZ - step):
                     send(
                         part,
                         part,
                         send_sem.at[3],
                         next_sem.at[index_of(c, here_p), half_line],
-                        peer(c, end),
+                        peer(c, (here_p + end) % NZ),
                     )
+            for half_line in range(2):
+                part = line(c, here_p, half_line)
                 send(
                     part,
                     part,
@@ -244,7 +245,6 @@
         @pl.when(core == c)
         def _(c=c):
             here_p = place_of(c)
-            ends = ((here_p + 1) % NZ, (here_p + NZ - 1) % NZ)
             steps = [(here_p, 0, 0, 0), (here_p, 0, 0, 1)] + [
                 (moved(c, d, way), d, way, half_line) for d, way, half_line in events
             ]
@@ -264,8 +264,10 @@
                 if d:
                     sem = next_sem.at[index_of(c, p), half_line]
                     await_bytes(part, sem)
-                    if d < 3 + (way == half_line):
-                        send(part, part, send_sem.at[3], sem, peer(c, ends[way]))
+                    if d == 2:
+                        for more in range(1, 2 + (way == half_line)):
+                            end = (here_p + (NZ - more if way else more)) % NZ
+                            send(part, part, send_sem.at[3], sem, peer(c, end))
                     send(
                         part,
                         part,
@@ -414,13 +416,16 @@
     await_bytes(z_mid.at[:, pl.ds(0, NS - 1)], send_sem.at[3])
 
 
-def spread(me, left_side, right_side, right_gates, a_out, rows_all, b_all, b_out, mids, l_sems, r_sems, x_sems):
+def spread(
+    me, left_side, right_side, right_gates, output_gates, a_out, rows_all, b_all, b_out, mids, l_sems, r_sems, x_sems
+):
     z, s, x = me.z, me.s, me.x
     ly_mid, lz_mid, ry_mid, rz_mid = mids
     x_send, near_sem, far_sem, side_sem = x_sems
     first_legs(me, left_side, ly_mid, lz_mid, l_sems[0], l_sems[1])
     right_gates()
     first_legs(me, right_side, ry_mid, rz_mid, r_sems[0], r_sems[1], (0,))
+    output_gates()
     left_legs(me, left_side, ly_mid, lz_mid, a_out.at[:, x], l_sems)
     first_legs(me, right_side, ry_mid, rz_mid, r_sems[0], r_sems[1], (1,))
 
@@ -487,11 +492,11 @@
         await_bytes(part, far_sem.at[n])
         await_bytes(part, near_sem.at[1 - k % 2, n])
 
-    @pl.loop(0, NX * NZ, unroll=2)
-    def _(k):
-        xt, zt = k // NZ, k % NZ
-        for h in range(2):
-            rows_all[xt, zt, :, lanes(h)] = flat_rows(a_out.at[h, xt, zt])
+    @pl.loop(0, NZ)
+    def _(zt):
+        for k in range(NX):
+            for h in range(2):
+                rows_all[zt, :, lanes(2 * k + h)] = flat_rows(a_out.at[h, k, zt])
 
     await_bytes(b_out, side_sem)
 
@@ -501,21 +506,22 @@
     z, s = me.z, me.s
     for k in range(NX):
         for h in range(2):
-            cols_all[k, :, lanes(h)] = flat_rows(b_out.at[h, k])
-    for t in ORDER:
-        zt = (z + t) % NZ
-        total = None
-        for k in range(NX):
-            term = lax.dot_general(
-                rows_all[k, zt], cols_all[k], (((1,), (1,)), ((), ())), preferred_element_type=F32
-            )
-            total = term if total is None else total + term
-        for h in range(2):
-            product[h, zt] = split_rows(total[:, lanes(h)])
-        if t == 0:
-            keep(product.at[1, z], z_mid.at[z], first_sem.at[1])
-        else:
-            send(product.at[1, zt], z_mid.at[z], send_sem.at[1], first_sem.at[1], me.at(z=zt))
+            cols_all[:, lanes(2 * k + h)] = flat_rows(b_out.at[h, k])
+    for couple in ((0, 1), (7, 2), (6, 3), (5, 4)):
+        rows = jnp.concatenate([rows_all[(z + t) % NZ] for t in couple], axis=0)
+        total = lax.dot_general(
+            rows, cols_all[...], (((1,), (1,)), ((), ())), preferred_element_type=F32
+        )
+        count = total.shape[0] // 2
+        for n, t in enumerate(couple):
+            zt = (z + t) % NZ
+            block = total[n * count : (n + 1) * count]
+            for h in range(2):
+                product[h, zt] = split_rows(block[:, lanes(h)])
+            if t == 0:
+                keep(product.at[1, z], z_mid.at[z], first_sem.at[1])
+            else:
+                send(product.at[1, zt], z_mid.at[z], send_sem.at[1], first_sem.at[1], me.at(z=zt))
     along_y(me, lambda st: product.at[0, :, st], y_mid.at[s], send_sem.at[0], first_sem.at[0])
     await_bytes(z_mid, first_sem.at[1])
     along_y(me, lambda st: z_mid.at[:, st], final.at[1, :, s], send_sem.at[3], final_sem)
@@ -524,21 +530,32 @@
     await_bytes(final, final_sem)
 
 
-def finish(parts, wide, mid_all, normed_all, gate_ref, out_ref, result):
+def output_gates(gate_ref, normed_all, gate_all):
+    gate = turned(gate_ref)
+
+    @pl.loop(0, normed_all.shape[0], unroll=2)
+    def _(i):
+        gate_all[i] = jax.nn.sigmoid(dot(gate, normed_all[i]))
+
+
+def finish(parts, wide, mid_all, gate_all, out_ref, rows_out, result, sem):
     rows, width, cols = mid_all.shape
     for h in range(2):
         wide[h] = parts[h].astype(F32).reshape(-1, 128)
     hidden = wide.shape[1] // rows
-    gate_w, out_w = turned(gate_ref), turned(out_ref)
-
-    @pl.loop(0, rows)
+    out_w = turned(out_ref)
+
+    @pl.loop(0, rows, unroll=4)
     def _(i):
         product = jnp.concatenate(
             [wide[h, pl.ds(i, hidden, stride=rows), :] for h in range(2)], axis=1
         )
         normed = layer_norm(product, 0).astype(BF16)
-        gate = jax.nn.sigmoid(dot(gate_w, normed_all[i]))
-        result[i] = (mid_all[i].astype(F32) + gate * dot(out_w, normed)).T.astype(BF16)
+        update = gate_all[i] * dot(out_w, normed)
+        rows_out[i] = (mid_all[i].astype(F32) + update).T.astype(BF16)
+        keep(rows_out.at[i], result.at[i], sem)
+
+    await_bytes(rows_out, sem)
 
 
 def kernel(
@@ -586,6 +603,8 @@
     cols_all,
     product,
     final,
+    gate_all,
+    rows_out,
     load_sem,
     g_send,
     g_first,
@@ -607,6 +626,7 @@
     p_send,
     p_first,
     p_final,
+    out_sem,
 ):
     me = Place()
     count = greet_all(me)
@@ -656,6 +676,7 @@
         lambda: right_gates(
             tri_right_gate_ref, tri_right_ref, normed_all, acc.at[1], right_side
         ),
+        lambda: output_gates(tri_gate_ref, normed_all, gate_all),
         a_out,
         rows_all,
         b_all,
@@ -668,7 +689,7 @@
     multiply_and_return(
         me, rows_all, b_out, cols_all, product, py_mid, pz_mid, final, (p_send, p_first, p_final)
     )
-    finish(final, acc.at[0], mid_all, normed_all, tri_gate_ref, tri_out_ref, result)
+    finish(final, acc.at[0], mid_all, gate_all, tri_out_ref, rows_out, result, out_sem)
     legs_left(ly_mid, lz_mid, l_send)
     legs_left(ry_mid, rz_mid, r_send)
     await_bytes(a_out.at[:, pl.ds(0, 2)], x_send.at[0])
@@ -718,11 +739,13 @@
         vb(NZ, NS, rows, 128),
         vb(2, NZ, NS, rows, 128),
         vb(2, NX, NZ, NS, rows, 128),
-        vb(NX, NZ, NS * rows, cols),
+        vb(NZ, NS * rows, NX * cols),
         vb(2, NX, NZ // NX, NS, rows, 128),
-        vb(NX, cols, cols),
+        vb(cols, NX * cols),
         vb(2, NZ, NS, rows, 128),
         vb(2, NZ, NS, rows, 128),
+        vf(rows, width, cols),
+        vb(rows, cols, width),
         DMA((2,)),
         DMA((5,)),
         DMA,
@@ -744,12 +767,13 @@
         DMA((4,)),
         DMA((2,)),
         DMA,
+        DMA,
     ]
     return pl.pallas_call(
         kernel,
         out_shape=jax.ShapeDtypeStruct((rows, cols, width), BF16),
         in_specs=[ANY, ANY] + [VMEM] * 9,
-        out_specs=VMEM,
+        out_specs=ANY,
         scratch_shapes=scratch,
         compiler_params=pltpu.CompilerParams(
             collective_id=0, has_side_effects=True, vmem_limit_bytes=56 << 20

time: 114 us -> 111 us (0.974)
  Pallas kernels: 111 us -> 109 us
    pallas_call x1, Pallas kernels: 111 us -> 109 us  [on_device(): pl.pallas_call(kernel, out_shape=jax.ShapeDtypeStruct((rows, cols, width)...]
where the time goes in v5:
time: 111 us
  Pallas kernels  109 us (98%)
  local copies, waits for them, and re-layouts  1.87 us (2%)
    pallas_call x1, Pallas kernels, on_device(): pl.pallas_call(kernel, out_shape=jax.ShapeDtypeStruct((rows, cols, width)...  109 us

profile of v5, /device:TPU:1, one launch (start us, length us, event | category | flops | bytes accessed | tf_op | source)
XLA Modules:
  0.0 110.9 jit_solution(2837358455694815645)
XLA Ops:
  0.0 109.0 %evoformer_pair.1 = bf16[8,256,128]{2,1,0:T(8,128)(2,1)} custom-call(bf16[8,256,128]{2,1,0:T(8,128)(2,1)} %pair_hbm.1, bf16[1024,128]{1,0:T(8,128)(2,1)} %opm_out_hbm.1, bf16[1,256,256]{2,1,0:T(8,128)(2,1)} %align_ref.1, bf16[32,256]{1,0:T(8,128)(2,1)} %bitcast.2, bf16[32,256]{1,0:T(8,128)(2,1)} %bitcast.3, bf16[128,128]{1,0:T(8,128)(2,1)} %tri_left_ref.1, ...), custom_call_target="tpu_custom_call" | custom-call | tf_op jit(solution)/shard_map/evoformer_pair/pallas_call | solution.py:772
  109.0 1.9 %copy.13 = bf16[8,256,128]{2,1,0:T(8,128)(2,1)} copy(bf16[8,256,128]{2,1,0:T(8,128)(2,1)} %evoformer_pair.1) | data formatting | bytes 1048576

commit v6 on v5

--- a/solution.py
+++ b/solution.py
@@ -310,14 +310,15 @@
             for h in range(2)
         ],
         axis=0,
-    ).astype(BF16)
+    )
+    left = (left * (1.0 / seqs)).astype(BF16)
 
     @pl.loop(0, factor, unroll=4)
     def _(q):
         part = jnp.concatenate(
             [wide[h, pl.ds(q, seqs, stride=factor), :] for h in range(2)], axis=1
         ).astype(BF16)
-        outer = dot(left, part) * (1.0 / seqs)
+        outer = dot(left, part)
         at = pl.ds(pl.multiple_of(q * factor, factor), factor)
         stack[:, at, :] = outer.astype(BF16).reshape(rows, factor, cols)
 
@@ -334,12 +335,12 @@
         side[h] = split_rows(acc[h]).reshape(side.shape[1:])
 
 
-def left_gates(out_w, pair, gate_ref, value_ref, stack, mid_all, normed_all, acc, side):
-    gate, value = turned(gate_ref), turned(value_ref)
+def left_gates(out_w, pair, gate, value, stack, mid_all, normed_all, acc, side):
+    gate, value = gate[...], value[...]
 
     @pl.loop(0, pair.shape[0], unroll=2)
     def _(i):
-        mid = (dot(out_w[...], stack[i]) + pair[i].astype(F32).T).astype(BF16)
+        mid = (dot(out_w[...], stack[i]) + pair[i]).astype(BF16)
         mid_all[i] = mid
         normed = layer_norm(mid, 0).astype(BF16)
         normed_all[i] = normed
@@ -348,8 +349,8 @@
     put_side(acc, side)
 
 
-def right_gates(gate_ref, value_ref, normed_all, acc, side):
-    gate, value = turned(gate_ref), turned(value_ref)
+def right_gates(gate, value, normed_all, acc, side):
+    gate, value = gate[...], value[...]
 
     @pl.loop(0, normed_all.shape[0], unroll=2)
     def _(i):
@@ -518,32 +519,69 @@
             block = total[n * count : (n + 1) * count]
             for h in range(2):
                 product[h, zt] = split_rows(block[:, lanes(h)])
-            if t == 0:
-                keep(product.at[1, z], z_mid.at[z], first_sem.at[1])
+    same = s // NQ * NQ
+    starts = (same, NQ - same)
+
+    def first(chunk):
+        near = pl.ds(pl.multiple_of(starts[chunk], NQ), NQ)
+        along_z(
+            me,
+            lambda zt: product.at[1, zt, near],
+            z_mid.at[z, near],
+            send_sem.at[1],
+            first_sem.at[1, chunk],
+        )
+        for t in range(chunk, NZ, 2):
+            zt = (z + t) % NZ
+            along_y(
+                me,
+                lambda st: product.at[0, zt, st],
+                y_mid.at[s, zt],
+                send_sem.at[0],
+                first_sem.at[0, chunk],
+            )
+
+    def second(chunk):
+        await_bytes(z_mid.at[:, pl.ds(0, NQ)], first_sem.at[1, chunk])
+        base = starts[chunk]
+        for t in range(NQ):
+            st = base + (s + t) % NQ
+            part, there = z_mid.at[:, st], final.at[1, :, s]
+            if t == 0 and chunk == 0:
+                keep(part, there, final_sem)
             else:
-                send(product.at[1, zt], z_mid.at[z], send_sem.at[1], first_sem.at[1], me.at(z=zt))
-    along_y(me, lambda st: product.at[0, :, st], y_mid.at[s], send_sem.at[0], first_sem.at[0])
-    await_bytes(z_mid, first_sem.at[1])
-    along_y(me, lambda st: z_mid.at[:, st], final.at[1, :, s], send_sem.at[3], final_sem)
-    await_bytes(y_mid, first_sem.at[0])
-    along_z(me, lambda zt: y_mid.at[:, zt], final.at[0, z], send_sem.at[2], final_sem)
+                send(part, there, send_sem.at[3], final_sem, me.at(s=st))
+        await_bytes(y_mid.at[:, pl.ds(0, NZ // 2)], first_sem.at[0, chunk])
+        along_z(
+            me,
+            lambda zt: y_mid.at[:, zt],
+            final.at[0, z],
+            send_sem.at[2],
+            final_sem,
+            (0, 2, 6, 4) if chunk == 0 else (1, 7, 3, 5),
+        )
+
+    first(0)
+    first(1)
+    second(0)
+    second(1)
     await_bytes(final, final_sem)
 
 
-def output_gates(gate_ref, normed_all, gate_all):
-    gate = turned(gate_ref)
+def output_gates(gate, normed_all, gate_all):
+    gate = gate[...]
 
     @pl.loop(0, normed_all.shape[0], unroll=2)
     def _(i):
         gate_all[i] = jax.nn.sigmoid(dot(gate, normed_all[i]))
 
 
-def finish(parts, wide, mid_all, gate_all, out_ref, rows_out, result, sem):
+def finish(parts, wide, mid_all, gate_all, out_w, rows_out, result, sem):
     rows, width, cols = mid_all.shape
     for h in range(2):
         wide[h] = parts[h].astype(F32).reshape(-1, 128)
     hidden = wide.shape[1] // rows
-    out_w = turned(out_ref)
+    out_w = out_w[...]
 
     @pl.loop(0, rows, unroll=4)
     def _(i):
@@ -605,6 +643,8 @@
     final,
     gate_all,
     rows_out,
+    pair_wide,
+    turned_all,
     load_sem,
     g_send,
     g_first,
@@ -643,6 +683,22 @@
         mine_rows = slice(k * p, (k + 1) * p)
         stack[0, mine_rows, 0:128] = rows.astype(BF16)
     out_w[...] = stack[0, :, 0:128].astype(F32).T.astype(BF16)
+    for k, ref in enumerate(
+        (
+            tri_left_ref,
+            tri_left_gate_ref,
+            tri_right_ref,
+            tri_right_gate_ref,
+            tri_gate_ref,
+            tri_out_ref,
+        )
+    ):
+        turned_all[k] = turned(ref)
+
+    @pl.loop(0, pair.shape[0])
+    def _(i):
+        pair_wide[i] = pair[i].astype(F32).T
+
     pl.semaphore_wait(pltpu.get_barrier_semaphore(), count)
 
     gather(
@@ -660,9 +716,9 @@
     outer_sums(mine, half_wide, wide, stack)
     left_gates(
         out_w,
-        pair,
-        tri_left_gate_ref,
-        tri_left_ref,
+        pair_wide,
+        turned_all.at[1],
+        turned_all.at[0],
         stack,
         mid_all,
         normed_all,
@@ -674,9 +730,9 @@
         left_side,
         right_side,
         lambda: right_gates(
-            tri_right_gate_ref, tri_right_ref, normed_all, acc.at[1], right_side
+            turned_all.at[3], turned_all.at[2], normed_all, acc.at[1], right_side
         ),
-        lambda: output_gates(tri_gate_ref, normed_all, gate_all),
+        lambda: output_gates(turned_all.at[4], normed_all, gate_all),
         a_out,
         rows_all,
         b_all,
@@ -689,7 +745,7 @@
     multiply_and_return(
         me, rows_all, b_out, cols_all, product, py_mid, pz_mid, final, (p_send, p_first, p_final)
     )
-    finish(final, acc.at[0], mid_all, gate_all, tri_out_ref, rows_out, result, out_sem)
+    finish(final, acc.at[0], mid_all, gate_all, turned_all.at[5], rows_out, result, out_sem)
     legs_left(ly_mid, lz_mid, l_send)
     legs_left(ry_mid, rz_mid, r_send)
     await_bytes(a_out.at[:, pl.ds(0, 2)], x_send.at[0])
@@ -746,6 +802,8 @@
         vb(2, NZ, NS, rows, 128),
         vf(rows, width, cols),
         vb(rows, cols, width),
+        vf(rows, width, cols),
+        vb(6, hidden, width),
         DMA((2,)),
         DMA((5,)),
         DMA,
@@ -765,7 +823,7 @@
         DMA((UNITS,)),
         DMA,
         DMA((4,)),
-        DMA((2,)),
+        DMA((2, 2)),
         DMA,
         DMA,
     ]

time: 111 us -> 109 us (0.982)
  Pallas kernels: 109 us -> 107 us
    pallas_call x1, Pallas kernels: 109 us -> 107 us  [on_device(): pl.pallas_call(kernel, out_shape=jax.ShapeDtypeStruct((rows, cols, width)...]
where the time goes in v6:
time: 109 us
  Pallas kernels  107 us (98%)
  local copies, waits for them, and re-layouts  1.87 us (2%)
    pallas_call x1, Pallas kernels, on_device(): pl.pallas_call(kernel, out_shape=jax.ShapeDtypeStruct((rows, cols, width)...  107 us

profile of v6, /device:TPU:1, one launch (start us, length us, event | category | flops | bytes accessed | tf_op | source)
XLA Modules:
  0.0 109.1 jit_solution(144013435530564653)
XLA Ops:
  0.0 107.2 %evoformer_pair.1 = bf16[8,256,128]{2,1,0:T(8,128)(2,1)} custom-call(bf16[8,256,128]{2,1,0:T(8,128)(2,1)} %pair_hbm.1, bf16[1024,128]{1,0:T(8,128)(2,1)} %opm_out_hbm.1, bf16[1,256,256]{2,1,0:T(8,128)(2,1)} %align_ref.1, bf16[32,256]{1,0:T(8,128)(2,1)} %bitcast.2, bf16[32,256]{1,0:T(8,128)(2,1)} %bitcast.3, bf16[128,128]{1,0:T(8,128)(2,1)} %tri_left_ref.1, ...), custom_call_target="tpu_custom_call" | custom-call | tf_op jit(solution)/shard_map/evoformer_pair/pallas_call | solution.py:830
  107.3 1.9 %copy.13 = bf16[8,256,128]{2,1,0:T(8,128)(2,1)} copy(bf16[8,256,128]{2,1,0:T(8,128)(2,1)} %evoformer_pair.1) | data formatting | bytes 1048576

commit v7 on v6

--- a/solution.py
+++ b/solution.py
@@ -576,7 +576,7 @@
         gate_all[i] = jax.nn.sigmoid(dot(gate, normed_all[i]))
 
 
-def finish(parts, wide, mid_all, gate_all, out_w, rows_out, result, sem):
+def finish(parts, wide, mid_all, gate_all, out_w, result):
     rows, width, cols = mid_all.shape
     for h in range(2):
         wide[h] = parts[h].astype(F32).reshape(-1, 128)
@@ -590,10 +590,7 @@
         )
         normed = layer_norm(product, 0).astype(BF16)
         update = gate_all[i] * dot(out_w, normed)
-        rows_out[i] = (mid_all[i].astype(F32) + update).T.astype(BF16)
-        keep(rows_out.at[i], result.at[i], sem)
-
-    await_bytes(rows_out, sem)
+        result[i] = (mid_all[i].astype(F32) + update).T.astype(BF16)
 
 
 def kernel(
@@ -642,7 +639,6 @@
     product,
     final,
     gate_all,
-    rows_out,
     pair_wide,
     turned_all,
     load_sem,
@@ -666,7 +662,6 @@
     p_send,
     p_first,
     p_final,
-    out_sem,
 ):
     me = Place()
     count = greet_all(me)
@@ -745,7 +740,7 @@
     multiply_and_return(
         me, rows_all, b_out, cols_all, product, py_mid, pz_mid, final, (p_send, p_first, p_final)
     )
-    finish(final, acc.at[0], mid_all, gate_all, turned_all.at[5], rows_out, result, out_sem)
+    finish(final, acc.at[0], mid_all, gate_all, turned_all.at[5], result)
     legs_left(ly_mid, lz_mid, l_send)
     legs_left(ry_mid, rz_mid, r_send)
     await_bytes(a_out.at[:, pl.ds(0, 2)], x_send.at[0])
@@ -801,7 +796,6 @@
         vb(2, NZ, NS, rows, 128),
         vb(2, NZ, NS, rows, 128),
         vf(rows, width, cols),
-        vb(rows, cols, width),
         vf(rows, width, cols),
         vb(6, hidden, width),
         DMA((2,)),
@@ -825,13 +819,12 @@
         DMA((4,)),
         DMA((2, 2)),
         DMA,
-        DMA,
     ]
     return pl.pallas_call(
         kernel,
-        out_shape=jax.ShapeDtypeStruct((rows, cols, width), BF16),
+        out_shape=pltpu.VMEM((rows, cols, width), BF16),
         in_specs=[ANY, ANY] + [VMEM] * 9,
-        out_specs=ANY,
+        out_specs=VMEM,
         scratch_shapes=scratch,
         compiler_params=pltpu.CompilerParams(
             collective_id=0, has_side_effects=True, vmem_limit_bytes=56 << 20

time: 109 us -> 108 us (level)
  no operation moved by 1% of the time
where the time goes in v7:
time: 108 us; the launch traced here: 107 us
  Pallas kernels  107 us (99%)
    pallas_call x1, Pallas kernels, on_device(): pl.pallas_call(kernel, out_shape=pltpu.VMEM((rows, cols, width), BF16), i...  107 us

profile of v7, /device:TPU:1, one launch (start us, length us, event | category | flops | bytes accessed | tf_op | source)
XLA Modules:
  0.0 107.4 jit_solution(421019090314055802)
XLA Ops:
  0.0 106.6 %evoformer_pair.1 = bf16[8,256,128]{2,1,0:T(8,128)(2,1)S(1)} custom-call(bf16[8,256,128]{2,1,0:T(8,128)(2,1)} %pair_hbm.1, bf16[1024,128]{1,0:T(8,128)(2,1)} %opm_out_hbm.1, bf16[1,256,256]{2,1,0:T(8,128)(2,1)} %align_ref.1, bf16[32,256]{1,0:T(8,128)(2,1)} %bitcast.2, bf16[32,256]{1,0:T(8,128)(2,1)} %bitcast.3, bf16[128,128]{1,0:T(8,128)(2,1)} %tri_left_ref.1, ...), custom_call_target="tpu_custom_call" | custom-call | tf_op jit(solution)/shard_map/evoformer_pair/pallas_call | solution.py:823
  106.6 0.8 copy.13
